TPU v7x, 32 devices: a whole 2x2x4 slice. The times are simulated.
32 devices in a mesh: dp: 4 (over z), pipe: 2 (over y), mp: 4 (over x, core).
Axes of the slice: x: 2, y: 2, z: 4, core: 2. Of those that a mesh axis runs over, the one named last changes fastest.
Arguments:
- fwd_in: bfloat16 [2, 512, 1024], P('pipe', ('dp', 'mp')), may hold values from -6 to 6
- grad_in: bfloat16 [2, 512, 1024], P('pipe', ('dp', 'mp')), may hold values from -6 to 6
- saved_in: bfloat16 [2, 512, 1024], P('pipe', ('dp', 'mp')), may hold values from -6 to 6
- saved_hidden: bfloat16 [2, 512, 65536], P('pipe', 'dp', 'mp'), may hold values from -6 to 6
- gain: float32 [2, 1024], P('pipe'), may hold values from 0.25 to 1.75
- w_in: bfloat16 [2, 1024, 65536], P('pipe', None, 'mp'), may hold values from -0.1875 to 0.1875
- w_out: bfloat16 [2, 65536, 1024], P('pipe', 'mp'), may hold values from -0.0234375 to 0.0234375
Outputs:
- fwd_out: bfloat16 [2, 512, 1024], P('pipe', ('dp', 'mp'))
- grad_out: bfloat16 [2, 512, 1024], P('pipe', ('dp', 'mp'))
All inputs are finite; a program needn't handle non-finite values.
Results may differ from a plain program's by a relative error of at most 0.008.
Values may be sent and summed in bfloat16 or wider, within the bound.
No kernel may reach another device: no remote copies, remote signals or barrier semaphores. Data moves between devices by JAX's collectives and lax.ppermute only.
A program may use at most 192 MiB of HBM per device.

v0:
```python
import jax
import jax.numpy as jnp
from jax import lax
from jax.sharding import PartitionSpec as P


def shifted(block, axis, distance):
    devices = range(lax.axis_size(axis))
    route = [((i - distance) % len(devices), i) for i in devices]
    return lax.ppermute(block, axis, route)


def on_device(fwd_in, grad_in, saved_in, saved_hidden, gain, w_in, w_out):
    scale = gain[0][None, :]
    weight_in = w_in[0]
    weight_out = w_out[0]
    active = saved_hidden[0] > 0
    xf = fwd_in[0].astype(jnp.float32)
    normed = (xf * lax.rsqrt(jnp.mean(xf * xf, axis=-1, keepdims=True) + 1e-06) * scale).astype(
        jnp.bfloat16
    )
    hidden = jnp.maximum(
        jnp.dot(
            lax.all_gather(normed, "mp", axis=0, tiled=True),
            weight_in,
            preferred_element_type=jnp.float32,
        ),
        0.0,
    ).astype(jnp.bfloat16)
    product = lax.dot_general(
        lax.all_gather(grad_in[0], "mp", axis=0, tiled=True),
        weight_out,
        (((1,), (1,)), ((), ())),
        preferred_element_type=jnp.float32,
    )
    hidden_grad = jnp.where(active, product, 0.0).astype(jnp.bfloat16)
    block = hidden
    projected = lax.psum_scatter(
        jnp.dot(block, weight_out, preferred_element_type=jnp.float32).astype(jnp.bfloat16),
        "mp",
        scatter_dimension=0,
        tiled=True,
    ).astype(jnp.float32)
    block = hidden_grad
    normed_grad = lax.psum_scatter(
        lax.dot_general(
            block, weight_in, (((1,), (1,)), ((), ())), preferred_element_type=jnp.float32
        ).astype(jnp.bfloat16),
        "mp",
        scatter_dimension=0,
        tiled=True,
    ).astype(jnp.float32)
    section_out = (xf + projected).astype(jnp.bfloat16)
    uf = saved_in[0].astype(jnp.float32)
    recip = lax.rsqrt(jnp.mean(uf * uf, axis=-1, keepdims=True) + 1e-06)
    scaled = normed_grad * scale
    inner = jnp.mean(scaled * uf, axis=-1, keepdims=True)
    input_grad = (
        grad_in[0].astype(jnp.float32) + recip * scaled - uf * recip * recip * recip * inner
    ).astype(jnp.bfloat16)
    moved_out = shifted(section_out, "pipe", 1)
    moved_grad = shifted(input_grad, "pipe", -1)
    return (moved_out[None], moved_grad[None])


def solution(mesh):
    in_specs = (
        P("pipe", ("dp", "mp"), None),
        P("pipe", ("dp", "mp"), None),
        P("pipe", ("dp", "mp"), None),
        P("pipe", "dp", "mp"),
        P("pipe", None),
        P("pipe", None, "mp"),
        P("pipe", "mp", None),
    )
    out_specs = (P("pipe", ("dp", "mp"), None), P("pipe", ("dp", "mp"), None))
    return jax.shard_map(
        on_device, mesh=mesh, in_specs=in_specs, out_specs=out_specs, check_vma=False
    )
```

profile of v0, /device:TPU:0, one launch (start us, length us, event | category | flops | bytes accessed | tf_op | source)
XLA Modules:
  0.0 131.3 jit_solution(4973882493033963061)
XLA Ops:
  7.2 0.0 reduce-scatter.5.cloned.1.call-start
  7.2 7.4 %all-gather = bf16[1,128,1024]{2,1,0:T(8,128)(2,1)S(1)} all-gather(bf16[1,32,1024]{2,1,0:T(8,128)(2,1)} %param.8), channel_id=2, replica_groups=mesh['dp'=4,'pipe'=2,'mp'=4] {'mp'}, dimensions={1}, use_global_device_ids=true | all-gather | bytes 327680 | tf_op jit(solution)/shard_map/all_gather | solution.py:31
  14.6 0.0 copy-start
  14.6 0.0 copy-start.2
  14.6 0.0 copy-start.3
  14.6 0.0 copy-start.1
  14.7 29.6 %fusion.25 = bf16[128,1024]{1,0:T(8,128)(2,1)} fusion(bf16[1,1024,16384]{2,1,0:T(8,128)(2,1)} %param.12, bf16[1,16384,1024]{2,1,0:T(8,128)(2,1)} %param.13, bf16[1,128,16384]{2,1,0:T(8,128)(2,1)} %param.10, bf16[1,128,1024]{2,1,0:T(8,128)(2,1)S(1)} %all-gather), kind=kOutput, calls=%fused_computation.13 | convolution fusion | flops 8596357120 | bytes 71827456 | tf_op jit(solution)/shard_map/dot_general | solution.py:46
  44.3 0.0 reduce-scatter.5.cloned.1.call-update
  44.3 0.0 reduce-scatter.3.cloned.1.call-start
  44.3 0.0 copy-done
  44.4 0.1 fusion.37
  44.5 21.3 %reduce-scatter.5.cloned.1.call-done = bf16[32,1024]{1,0:T(8,128)(2,1)} async-done(((bf16[128,1024]{1,0:T(8,128)(2,1)}), bf16[32,1024]{1,0:T(8,128)(2,1)}) %reduce-scatter.5.cloned.1.call-update) | async-done | bytes 65552 | tf_op jit(solution)/shard_map/reduce_scatter | solution.py:45
  65.8 0.0 copy-done.2
  65.8 0.0 copy-done.3
  65.8 1.0 fusion.41
  66.8 0.0 copy-done.1
  66.8 1.0 fusion.46
  67.8 5.8 %all_gather.6 = bf16[128,1024]{1,0:T(8,128)(2,1)S(1)} all-gather(bf16[32,1024]{1,0:T(8,128)(2,1)S(1)} %get-tuple-element.5), channel_id=1, replica_groups=mesh['dp'=4,'pipe'=2,'mp'=4] {'mp'}, dimensions={0}, use_global_device_ids=true | all-gather | bytes 327680 | tf_op jit(solution)/shard_map/all_gather | solution.py:24
  73.6 24.2 %fusion.30 = bf16[128,1024]{1,0:T(8,128)(2,1)} fusion(bf16[1,16384,1024]{2,1,0:T(8,128)(2,1)} %param.13, bf16[128,1024]{1,0:T(8,128)(2,1)S(1)} %all_gather.6, bf16[1,1024,16384]{2,1,0:T(8,128)(2,1)} %param.12), kind=kOutput, calls=%fused_computation.14 | convolution fusion | flops 8594259968 | bytes 67633152 | tf_op jit(solution)/shard_map/dot_general | solution.py:39
  97.8 0.0 reduce-scatter.3.cloned.1.call-update
  97.8 1.5 %collective-permute-start.1 = (bf16[32,1024]{1,0:T(8,128)(2,1)S(1)}, bf16[32,1024]{1,0:T(8,128)(2,1)S(1)}, u32[]{:S(2)}, u32[]{:S(2)}) collective-permute-start(bf16[32,1024]{1,0:T(8,128)(2,1)S(1)} %get-tuple-element.4), channel_id=1, source_target_pairs={{4,0},{0,4},{5,1},{1,5},{6,2},{2,6},{7,3},{3,7},{12,8},{8,12},{13,... | collective-permute-start | bytes 196616 | tf_op jit(solution)/shard_map/ppermute | solution.py:10
  99.4 18.7 %reduce-scatter.3.cloned.1.call-done = bf16[32,1024]{1,0:T(8,128)(2,1)} async-done(((bf16[128,1024]{1,0:T(8,128)(2,1)}), bf16[32,1024]{1,0:T(8,128)(2,1)}) %reduce-scatter.3.cloned.1.call-update) | async-done | bytes 65552 | tf_op jit(solution)/shard_map/reduce_scatter | solution.py:38
  118.0 0.9 fusion.40
  118.9 1.5 %collective-permute-start = (bf16[32,1024]{1,0:T(8,128)(2,1)S(1)}, bf16[32,1024]{1,0:T(8,128)(2,1)S(1)}, u32[]{:S(2)}, u32[]{:S(2)}) collective-permute-start(bf16[32,1024]{1,0:T(8,128)(2,1)S(1)} %fusion.40), channel_id=1, source_target_pairs={{4,0},{0,4},{5,1},{1,5},{6,2},{2,6},{7,3},{3,7},{12,8},{8,12},{13,... | collective-permute-start | bytes 196616 | tf_op jit(solution)/shard_map/ppermute | solution.py:10
  120.4 0.0 collective-permute-done.1
  120.4 2.8 %collective-permute-done = bf16[32,1024]{1,0:T(8,128)(2,1)S(1)} collective-permute-done((bf16[32,1024]{1,0:T(8,128)(2,1)S(1)}, bf16[32,1024]{1,0:T(8,128)(2,1)S(1)}, u32[]{:S(2)}, u32[]{:S(2)}) %collective-permute-start) | collective-permute-done | bytes 65568 | tf_op jit(solution)/shard_map/ppermute | solution.py:10
  123.2 0.6 copy.11
  123.9 0.6 copy.12
  (2 shorter events, 0.0 us)
Async XLA Ops:
  7.2 58.6 %reduce-scatter.5.cloned.1.call-start = ((), (), s32[]{:S(2)}) async-start(), calls=%async_computation.3 | async-start | bytes 327680 | tf_op jit(solution)/shard_map/reduce_scatter | solution.py:45
  14.6 29.7 %copy-start = (bf16[1,32,1024]{2,1,0:T(8,128)(2,1)S(1)}, bf16[1,32,1024]{2,1,0:T(8,128)(2,1)}, u32[]{:S(2)}) copy-start(bf16[1,32,1024]{2,1,0:T(8,128)(2,1)} %param.7) | copy-start | bytes 196612
  14.6 51.2 %copy-start.2 = (bf16[1,32,1024]{2,1,0:T(8,128)(2,1)S(1)}, bf16[1,32,1024]{2,1,0:T(8,128)(2,1)}, u32[]{:S(2)}) copy-start(bf16[1,32,1024]{2,1,0:T(8,128)(2,1)} %param.9) | copy-start | bytes 196612
  14.6 51.2 %copy-start.3 = (f32[1,1024]{1,0:T(1,128)S(1)}, f32[1,1024]{1,0:T(1,128)}, u32[]{:S(2)}) copy-start(f32[1,1024]{1,0:T(1,128)} %param.11) | copy-start | bytes 12292
  14.6 52.1 %copy-start.1 = (bf16[1,32,1024]{2,1,0:T(8,128)(2,1)S(1)}, bf16[1,32,1024]{2,1,0:T(8,128)(2,1)}, u32[]{:S(2)}) copy-start(bf16[1,32,1024]{2,1,0:T(8,128)(2,1)} %param.8) | copy-start | bytes 196612
  44.3 73.7 %reduce-scatter.3.cloned.1.call-start = ((), (), s32[]{:S(2)}) async-start(), calls=%async_computation.2 | async-start | bytes 327680 | tf_op jit(solution)/shard_map/reduce_scatter | solution.py:38
  97.8 22.6 %collective-permute-start.1 = (bf16[32,1024]{1,0:T(8,128)(2,1)S(1)}, bf16[32,1024]{1,0:T(8,128)(2,1)S(1)}, u32[]{:S(2)}, u32[]{:S(2)}) collective-permute-start(bf16[32,1024]{1,0:T(8,128)(2,1)S(1)} %get-tuple-element.4), channel_id=1, source_target_pairs={{4,0},{0,4},{5,1},{1,5},{6,2},{2,6},{7,3},{3,7},{12,8},{8,12},{13,... | collective-permute-start | bytes 196616 | tf_op jit(solution)/shard_map/ppermute | solution.py:10
  118.9 4.3 %collective-permute-start = (bf16[32,1024]{1,0:T(8,128)(2,1)S(1)}, bf16[32,1024]{1,0:T(8,128)(2,1)S(1)}, u32[]{:S(2)}, u32[]{:S(2)}) collective-permute-start(bf16[32,1024]{1,0:T(8,128)(2,1)S(1)} %fusion.40), channel_id=1, source_target_pairs={{4,0},{0,4},{5,1},{1,5},{6,2},{2,6},{7,3},{3,7},{12,8},{8,12},{13,... | collective-permute-start | bytes 196616 | tf_op jit(solution)/shard_map/ppermute | solution.py:10
Sparse Core Ops, SparseCore 0:
  44.4 21.3 reduce-scatter.4
  97.9 20.0 reduce-scatter.2
where the time goes:
time: 132 us; the launch traced here: 131 us
  matrix products  53.9 us (41%)
  waiting for transfers between devices  42.8 us (32%)
  between operations  14.1 us (11%)
  blocking collectives  13.2 us (10%)
  starting transfers between devices  3.15 us (2%)
  other arithmetic  2.94 us (2%)
    dot_general x1, matrix products, on_device(): lax.dot_general(block, weight_in, (((1,), (1,)), ((), ())), preferred_ele...  29.6 us
    dot_general x1, matrix products, on_device(): jnp.dot(block, weight_out, preferred_element_type=jnp.float32)  24.2 us
    reduce_scatter x1, waiting for transfers between devices, on_device(): lax.psum_scatter(lax.dot_general(block, weight_in, (((1,), (1,)), ((), ()...  21.3 us
    reduce_scatter x1, waiting for transfers between devices, on_device(): lax.psum_scatter(jnp.dot(block, weight_out, preferred_element_type=jnp.fl...  18.7 us
    all_gather x1, blocking collectives, on_device(): lax.all_gather(grad_in[0], 'mp', axis=0, tiled=True)  7.43 us
    all_gather x1, blocking collectives, on_device(): lax.all_gather(normed, 'mp', axis=0, tiled=True)  5.78 us
    ppermute x2, starting transfers between devices, shifted(): return lax.ppermute(block, axis, route)  3.07 us
    ppermute x2, waiting for transfers between devices, shifted(): return lax.ppermute(block, axis, route)  2.8 us
  transfers between devices with their start and end apart: 4, of which 3 were waited for; matrix products, arithmetic and copies ran while one was open for 1% of the time, Pallas kernels for 0%

commit v1 on v0

v1 whole, which is shorter than its diff:
```python
import functools

import jax
import jax.numpy as jnp
from jax import lax
from jax.experimental import pallas as pl
from jax.experimental.pallas import tpu as pltpu
from jax.sharding import PartitionSpec as P

EPS = 1e-06
NT = (((1,), (1,)), ((), ()))
F32 = jnp.float32
BF16 = jnp.bfloat16


def tile_of(extent, limit):
    size = limit
    while size > 128 and extent % size:
        size //= 2
    return size if extent % size == 0 else extent


def section_kernel(tiles, x_ref, g_ref, scale_ref, s_ref, wi_ref, wo_ref, of_ref, ob_ref, n_ref, af, ab):
    step = pl.program_id(0)

    @pl.when(step == 0)
    def _():
        xf = x_ref[...].astype(F32)
        r = lax.rsqrt(jnp.mean(xf * xf, axis=-1, keepdims=True) + EPS)
        n_ref[...] = (xf * r * scale_ref[...]).astype(BF16)
        af[...] = jnp.zeros_like(af)
        ab[...] = jnp.zeros_like(ab)

    h = jnp.maximum(jnp.dot(n_ref[...], wi_ref[...], preferred_element_type=F32), 0.0).astype(BF16)
    af[...] += jnp.dot(h, wo_ref[...], preferred_element_type=F32)
    p = lax.dot_general(g_ref[...], wo_ref[...], NT, preferred_element_type=F32)
    hg = jnp.where(s_ref[...] > 0, p, 0.0).astype(BF16)
    ab[...] += lax.dot_general(hg, wi_ref[...], NT, preferred_element_type=F32)

    @pl.when(step == tiles - 1)
    def _():
        of_ref[...] = af[...].astype(BF16)
        ob_ref[...] = ab[...].astype(BF16)


def section(x, g, scale, saved, w_in, w_out):
    tokens, width = x.shape
    hidden = w_in.shape[1]
    tile = tile_of(hidden, 1024)
    tiles = hidden // tile
    whole = pl.BlockSpec((tokens, width), lambda i: (0, 0))
    out = jax.ShapeDtypeStruct((tokens, width), BF16)
    return pl.pallas_call(
        functools.partial(section_kernel, tiles),
        grid=(tiles,),
        in_specs=[
            whole,
            whole,
            pl.BlockSpec((1, width), lambda i: (0, 0)),
            pl.BlockSpec((tokens, tile), lambda i: (0, i)),
            pl.BlockSpec((width, tile), lambda i: (0, i)),
            pl.BlockSpec((tile, width), lambda i: (i, 0)),
        ],
        out_specs=[whole, whole],
        out_shape=[out, out],
        scratch_shapes=[
            pltpu.VMEM((tokens, width), BF16),
            pltpu.VMEM((tokens, width), F32),
            pltpu.VMEM((tokens, width), F32),
        ],
        compiler_params=pltpu.CompilerParams(
            dimension_semantics=("arbitrary",), vmem_limit_bytes=48 << 20
        ),
        cost_estimate=pl.CostEstimate(
            flops=8 * tokens * width * hidden,
            bytes_accessed=4 * width * hidden + 2 * tokens * hidden,
            transcendentals=0,
        ),
        name="section",
    )(x, g, scale, saved, w_in, w_out)


def shifted(block, axis, distance):
    devices = range(lax.axis_size(axis))
    route = [((i - distance) % len(devices), i) for i in devices]
    return lax.ppermute(block, axis, route)


def gathered(block, axis):
    size = lax.axis_size(axis)
    rows = block.shape[0]
    me = lax.axis_index(axis)
    full = jnp.zeros((size * rows,) + block.shape[1:], block.dtype)
    full = lax.dynamic_update_slice(full, block, (me * rows, 0))
    for distance in range(1, size):
        got = shifted(block, axis, distance)
        full = lax.dynamic_update_slice(full, got, (((me - distance) % size) * rows, 0))
    return full


def scattered(full, axis):
    size = lax.axis_size(axis)
    rows = full.shape[0] // size
    me = lax.axis_index(axis)
    total = lax.dynamic_slice(full, (me * rows, 0), (rows, full.shape[1])).astype(F32)
    for distance in range(1, size):
        part = lax.dynamic_slice(full, (((me + distance) % size) * rows, 0), (rows, full.shape[1]))
        total = total + shifted(part, axis, distance).astype(F32)
    return total


def on_device(fwd_in, grad_in, saved_in, saved_hidden, gain, w_in, w_out):
    scale = gain[0][None, :]
    x, g, u = fwd_in[0], grad_in[0], saved_in[0]
    out_part, grad_part = section(
        gathered(x, "mp"), gathered(g, "mp"), scale, saved_hidden[0], w_in[0], w_out[0]
    )
    projected = scattered(out_part, "mp")
    normed_grad = scattered(grad_part, "mp")
    section_out = (x.astype(F32) + projected).astype(BF16)
    uf = u.astype(F32)
    recip = lax.rsqrt(jnp.mean(uf * uf, axis=-1, keepdims=True) + EPS)
    scaled = normed_grad * scale
    inner = jnp.mean(scaled * uf, axis=-1, keepdims=True)
    input_grad = (g.astype(F32) + recip * scaled - uf * recip * recip * recip * inner).astype(BF16)
    return (shifted(section_out, "pipe", 1)[None], shifted(input_grad, "pipe", -1)[None])


def solution(mesh):
    rows = P("pipe", ("dp", "mp"), None)
    in_specs = (
        rows,
        rows,
        rows,
        P("pipe", "dp", "mp"),
        P("pipe", None),
        P("pipe", None, "mp"),
        P("pipe", "mp", None),
    )
    return jax.shard_map(
        on_device, mesh=mesh, in_specs=in_specs, out_specs=(rows, rows), check_vma=False
    )
```

time: 132 us -> 66.6 us (0.50)
  matrix products: 53.9 us -> 0 us
  Pallas kernels: 0 us -> 37.6 us
  waiting for transfers between devices: 42.8 us -> 6.75 us
  between operations: 14.1 us -> 0.76 us
  blocking collectives: 13.2 us -> 0 us
  starting transfers between devices: 3.15 us -> 14.8 us
  local copies, waits for them, and re-layouts: 1.27 us -> 5.98 us
  other arithmetic: 2.94 us -> 0.34 us
    dot_general x2 -> x0, matrix products: 53.9 us -> none  [the longest x1 29.6 us: on_device(): lax.dot_general(block, weight_in, (((1,), (1,)), ((), ())), preferred_ele...]
    reduce_scatter x2 -> x0, waiting for transfers between devices: 40 us -> none  [the longest x1 21.3 us: on_device(): lax.psum_scatter(lax.dot_general(block, weight_in, (((1,), (1,)), ((), ()...]
    pallas_call x0 -> x1, Pallas kernels: none -> 37.6 us  [section(): pl.pallas_call(functools.partial(section_kernel, tiles), grid=(tiles,), i...]
    all_gather x2 -> x0, blocking collectives: 13.2 us -> none  [the longest x1 7.43 us: on_device(): lax.all_gather(grad_in[0], 'mp', axis=0, tiled=True)]
    ppermute x2 -> x14, starting transfers between devices: 3.07 us -> 14.8 us  [shifted(): return lax.ppermute(block, axis, route)]
    ppermute x2 -> x14, waiting for transfers between devices: 2.8 us -> 6.75 us  [shifted(): return lax.ppermute(block, axis, route)]
    unnamed x10 -> x12, local copies, waits for them, and re-layouts: 1.27 us -> 4.14 us
    dynamic_update_slice x0 -> x8, local copies, waits for them, and re-layouts: none -> 1.76 us  [the longest x2 1.7 us: gathered(): full = lax.dynamic_update_slice(full, block, (me * rows, 0))]
  transfers between devices with their start and end apart: 4 -> 14, of which waited for: 3 -> 7; matrix products, arithmetic and copies ran while one was open for 1% -> 3% of each run, Pallas kernels for 0% -> 0%
where the time goes in v1:
time: 66.6 us; the launch traced here: 66.3 us
  Pallas kernels  37.6 us (56%)
  starting transfers between devices  14.8 us (22%)
  waiting for transfers between devices  6.75 us (10%)
  local copies, waits for them, and re-layouts  5.98 us (9%)
  between operations  0.76 us (1%)
    pallas_call x1, Pallas kernels, section(): pl.pallas_call(functools.partial(section_kernel, tiles), grid=(tiles,), i...  37.6 us
    ppermute x14, starting transfers between devices, shifted(): return lax.ppermute(block, axis, route)  14.8 us
    ppermute x14, waiting for transfers between devices, shifted(): return lax.ppermute(block, axis, route)  6.75 us
    unnamed x12, local copies, waits for them, and re-layouts  4.14 us
    dynamic_update_slice x2, local copies, waits for them, and re-layouts, gathered(): full = lax.dynamic_update_slice(full, block, (me * rows, 0))  1.7 us
  transfers between devices with their start and end apart: 14, of which 7 were waited for; matrix products, arithmetic and copies ran while one was open for 3% of the time, Pallas kernels for 0%

profile of v1, /device:TPU:0, one launch (start us, length us, event | category | flops | bytes accessed | tf_op | source)
XLA Modules:
  0.0 66.3 jit_solution(12853706948831192653)
XLA Ops:
  0.6 0.5 collective-permute-start.3
  1.2 2.6 %collective-permute-start.4 = (bf16[32,1024]{1,0:T(8,128)(2,1)}, bf16[32,1024]{1,0:T(8,128)(2,1)S(1)}, u32[]{:S(2)}, u32[]{:S(2)}) collective-permute-start(bf16[32,1024]{1,0:T(8,128)(2,1)} %bitcast.23), channel_id=1, source_target_pairs={{2,0},{3,1},{0,2},{1,3},{6,4},{7,5},{4,6},{5,7},{10,8},{11,9},{8,1... | collective-permute-start | bytes 196616 | tf_op jit(solution)/shard_map/ppermute | solution.py:86
  3.7 1.4 %collective-permute-start.5 = (bf16[32,1024]{1,0:T(8,128)(2,1)}, bf16[32,1024]{1,0:T(8,128)(2,1)S(1)}, u32[]{:S(2)}, u32[]{:S(2)}) collective-permute-start(bf16[32,1024]{1,0:T(8,128)(2,1)} %bitcast.24), channel_id=1, source_target_pairs={{1,0},{2,1},{3,2},{0,3},{5,4},{6,5},{7,6},{4,7},{9,8},{10,9},{11,1... | collective-permute-start | bytes 196616 | tf_op jit(solution)/shard_map/ppermute | solution.py:86
  5.1 0.0 collective-permute-start
  5.1 0.4 collective-permute-start.1
  5.5 0.9 %constant_dynamic-update-slice_fusion.3 = bf16[128,1024]{1,0:T(8,128)(2,1)S(1)} fusion(bf16[128,1024]{1,0:T(8,128)(2,1)S(1)} %broadcast.29.clone.1, s32[]{:T(128)S(6)} %select_n.69, bf16[1,32,1024]{2,1,0:T(8,128)(2,1)} %param.8), kind=kLoop, calls=%fused_computation.21 | loop fusion | bytes 131076 | tf_op jit(solution)/shard_map/dynamic_update_slice | solution.py:94
  6.4 0.9 %constant_dynamic-update-slice_fusion.7 = bf16[128,1024]{1,0:T(8,128)(2,1)S(1)} fusion(bf16[128,1024]{1,0:T(8,128)(2,1)S(1)} %broadcast.29.clone, s32[]{:T(128)S(6)} %select_n.69, bf16[1,32,1024]{2,1,0:T(8,128)(2,1)} %param.7), kind=kLoop, calls=%fused_computation.25 | loop fusion | bytes 131076 | tf_op jit(solution)/shard_map/dynamic_update_slice | solution.py:94
  7.3 0.0 collective-permute-done.3
  7.3 1.4 %collective-permute-start.2 = (bf16[32,1024]{1,0:T(8,128)(2,1)}, bf16[32,1024]{1,0:T(8,128)(2,1)S(1)}, u32[]{:S(2)}, u32[]{:S(2)}) collective-permute-start(bf16[32,1024]{1,0:T(8,128)(2,1)} %bitcast.27), channel_id=1, source_target_pairs={{1,0},{2,1},{3,2},{0,3},{5,4},{6,5},{7,6},{4,7},{9,8},{10,9},{11,1... | collective-permute-start | bytes 196616 | tf_op jit(solution)/shard_map/ppermute | solution.py:86
  8.7 0.5 collective-permute-done
  9.1 0.0 collective-permute-done.4
  9.2 1.1 %collective-permute-done.1 = bf16[32,1024]{1,0:T(8,128)(2,1)S(1)} collective-permute-done((bf16[32,1024]{1,0:T(8,128)(2,1)}, bf16[32,1024]{1,0:T(8,128)(2,1)S(1)}, u32[]{:S(2)}, u32[]{:S(2)}) %collective-permute-start.1) | collective-permute-done | bytes 65568 | tf_op jit(solution)/shard_map/ppermute | solution.py:86
  10.3 0.0 collective-permute-done.5
  10.3 0.6 collective-permute-done.2
  10.9 0.0 copy-start
  10.9 2.2 %copy-done = bf16[1,128,16384]{2,1,0:T(8,128)(2,1)S(1)} copy-done((bf16[1,128,16384]{2,1,0:T(8,128)(2,1)S(1)}, bf16[1,128,16384]{2,1,0:T(8,128)(2,1)}, u32[]{:S(2)}) %copy-start) | copy-done | bytes 4194328
  13.1 0.0 copy-start.1
  13.1 0.7 %copy-done.1 = f32[1,1024]{1,0:T(1,128)S(1)} copy-done((f32[1,1024]{1,0:T(1,128)S(1)}, f32[1,1024]{1,0:T(1,128)}, u32[]{:S(2)}) %copy-start.1) | copy-done | bytes 4120
  13.8 0.0 copy-start.4
  13.8 0.0 copy-start.2
  13.8 0.0 copy-start.3
  13.8 37.6 %section.1 = (bf16[128,1024]{1,0:T(8,128)(2,1)S(1)}, bf16[128,1024]{1,0:T(8,128)(2,1)S(1)}) custom-call(bf16[128,1024]{1,0:T(8,128)(2,1)S(1)} %constant_dynamic-update-slice_fusion.4.x_ref, bf16[128,1024]{1,0:T(8,128)(2,1)S(1)} %constant_dynamic-update-slice_fusion.g_ref, f32[1,1024]{1,0:T(1,128)S(1)} %copy-done.1, bf16[128,16384]{1,0:T(8,128)(2,1)S(1)} %bitcast.17, ...), custom_call_target="tpu_custom_call" | custom-call | flops 17179869184 | bytes 71303168 | tf_op jit(solution)/shard_map/section/pallas_call | solution.py:53
  51.4 1.8 %collective-permute-start.10 = (bf16[32,1024]{1,0:T(8,128)(2,1)S(1)}, bf16[32,1024]{1,0:T(8,128)(2,1)S(1)}, u32[]{:S(2)}, u32[]{:S(2)}) collective-permute-start(bf16[32,1024]{1,0:T(8,128)(2,1)S(1)} %get-tuple-element.8), channel_id=1, source_target_pairs={{3,0},{0,1},{1,2},{2,3},{7,4},{4,5},{5,6},{6,7},{11,8},{8,9},{9,10... | collective-permute-start | bytes 196616 | tf_op jit(solution)/shard_map/ppermute | solution.py:86
  53.3 0.3 collective-permute-start.11
  53.6 1.1 %collective-permute-start.12 = (bf16[32,1024]{1,0:T(8,128)(2,1)S(1)}, bf16[32,1024]{1,0:T(8,128)(2,1)S(1)}, u32[]{:S(2)}, u32[]{:S(2)}) collective-permute-start(bf16[32,1024]{1,0:T(8,128)(2,1)S(1)} %get-tuple-element.9), channel_id=1, source_target_pairs={{1,0},{2,1},{3,2},{0,3},{5,4},{6,5},{7,6},{4,7},{9,8},{10,9},{11,1... | collective-permute-start | bytes 196616 | tf_op jit(solution)/shard_map/ppermute | solution.py:86
  54.7 0.1 collective-permute-start.6
  54.8 1.1 %collective-permute-start.7 = (bf16[32,1024]{1,0:T(8,128)(2,1)S(1)}, bf16[32,1024]{1,0:T(8,128)(2,1)S(1)}, u32[]{:S(2)}, u32[]{:S(2)}) collective-permute-start(bf16[32,1024]{1,0:T(8,128)(2,1)S(1)} %get-tuple-element.13), channel_id=1, source_target_pairs={{2,0},{3,1},{0,2},{1,3},{6,4},{7,5},{4,6},{5,7},{10,8},{11,9},{8,1... | collective-permute-start | bytes 196616 | tf_op jit(solution)/shard_map/ppermute | solution.py:86
  55.9 0.0 collective-permute-done.10
  55.9 1.0 %collective-permute-start.8 = (bf16[32,1024]{1,0:T(8,128)(2,1)S(1)}, bf16[32,1024]{1,0:T(8,128)(2,1)S(1)}, u32[]{:S(2)}, u32[]{:S(2)}) collective-permute-start(bf16[32,1024]{1,0:T(8,128)(2,1)S(1)} %get-tuple-element.12), channel_id=1, source_target_pairs={{1,0},{2,1},{3,2},{0,3},{5,4},{6,5},{7,6},{4,7},{9,8},{10,9},{11,1... | collective-permute-start | bytes 196616 | tf_op jit(solution)/shard_map/ppermute | solution.py:86
  56.9 0.7 %collective-permute-done.11 = bf16[32,1024]{1,0:T(8,128)(2,1)S(1)} collective-permute-done((bf16[32,1024]{1,0:T(8,128)(2,1)S(1)}, bf16[32,1024]{1,0:T(8,128)(2,1)S(1)}, u32[]{:S(2)}, u32[]{:S(2)}) %collective-permute-start.11) | collective-permute-done | bytes 65568 | tf_op jit(solution)/shard_map/ppermute | solution.py:86
  57.6 0.0 collective-permute-done.12
  57.6 0.0 copy-done.4
  57.6 0.2 fusion
  57.7 0.0 copy-done.2
  57.7 0.1 fusion.5
  57.9 1.6 %collective-permute-start.13 = (bf16[32,1024]{1,0:T(8,128)(2,1)S(1)}, bf16[32,1024]{1,0:T(8,128)(2,1)S(1)}, u32[]{:S(2)}, u32[]{:S(2)}) collective-permute-start(bf16[32,1024]{1,0:T(8,128)(2,1)S(1)} %fusion.5), channel_id=1, source_target_pairs={{4,0},{0,4},{5,1},{1,5},{6,2},{2,6},{7,3},{3,7},{12,8},{8,12},{13,... | collective-permute-start | bytes 196616 | tf_op jit(solution)/shard_map/ppermute | solution.py:86
  59.4 0.0 collective-permute-done.6
  59.5 0.7 %collective-permute-done.7 = bf16[32,1024]{1,0:T(8,128)(2,1)S(1)} collective-permute-done((bf16[32,1024]{1,0:T(8,128)(2,1)S(1)}, bf16[32,1024]{1,0:T(8,128)(2,1)S(1)}, u32[]{:S(2)}, u32[]{:S(2)}) %collective-permute-start.7) | collective-permute-done | bytes 65568 | tf_op jit(solution)/shard_map/ppermute | solution.py:86
  60.1 0.0 collective-permute-done.8
  60.1 0.0 copy-done.3
  60.1 0.1 add_convert_fusion
  60.2 1.6 %collective-permute-start.9 = (bf16[32,1024]{1,0:T(8,128)(2,1)S(1)}, bf16[32,1024]{1,0:T(8,128)(2,1)S(1)}, u32[]{:S(2)}, u32[]{:S(2)}) collective-permute-start(bf16[32,1024]{1,0:T(8,128)(2,1)S(1)} %add_convert_fusion), channel_id=1, source_target_pairs={{4,0},{0,4},{5,1},{1,5},{6,2},{2,6},{7,3},{3,7},{12,8},{8,12},{13,... | collective-permute-start | bytes 196616 | tf_op jit(solution)/shard_map/ppermute | solution.py:86
  61.8 0.8 %collective-permute-done.13 = bf16[32,1024]{1,0:T(8,128)(2,1)S(1)} collective-permute-done((bf16[32,1024]{1,0:T(8,128)(2,1)S(1)}, bf16[32,1024]{1,0:T(8,128)(2,1)S(1)}, u32[]{:S(2)}, u32[]{:S(2)}) %collective-permute-start.13) | collective-permute-done | bytes 65568 | tf_op jit(solution)/shard_map/ppermute | solution.py:86
  62.6 2.4 %collective-permute-done.9 = bf16[32,1024]{1,0:T(8,128)(2,1)S(1)} collective-permute-done((bf16[32,1024]{1,0:T(8,128)(2,1)S(1)}, bf16[32,1024]{1,0:T(8,128)(2,1)S(1)}, u32[]{:S(2)}, u32[]{:S(2)}) %collective-permute-start.9) | collective-permute-done | bytes 65568 | tf_op jit(solution)/shard_map/ppermute | solution.py:86
  65.0 0.6 copy.19
  65.6 0.6 copy.20
  (11 shorter events, 0.1 us)
Async XLA Ops:
  0.6 6.6 %collective-permute-start.3 = (bf16[32,1024]{1,0:T(8,128)(2,1)}, bf16[32,1024]{1,0:T(8,128)(2,1)S(1)}, u32[]{:S(2)}, u32[]{:S(2)}) collective-permute-start(bf16[32,1024]{1,0:T(8,128)(2,1)} %bitcast.22), channel_id=1, source_target_pairs={{3,0},{0,1},{1,2},{2,3},{7,4},{4,5},{5,6},{6,7},{11,8},{8,9},{9,10... | collective-permute-start | bytes 196616 | tf_op jit(solution)/shard_map/ppermute | solution.py:86
  1.2 8.0 %collective-permute-start.4 = (bf16[32,1024]{1,0:T(8,128)(2,1)}, bf16[32,1024]{1,0:T(8,128)(2,1)S(1)}, u32[]{:S(2)}, u32[]{:S(2)}) collective-permute-start(bf16[32,1024]{1,0:T(8,128)(2,1)} %bitcast.23), channel_id=1, source_target_pairs={{2,0},{3,1},{0,2},{1,3},{6,4},{7,5},{4,6},{5,7},{10,8},{11,9},{8,1... | collective-permute-start | bytes 196616 | tf_op jit(solution)/shard_map/ppermute | solution.py:86
  3.7 6.6 %collective-permute-start.5 = (bf16[32,1024]{1,0:T(8,128)(2,1)}, bf16[32,1024]{1,0:T(8,128)(2,1)S(1)}, u32[]{:S(2)}, u32[]{:S(2)}) collective-permute-start(bf16[32,1024]{1,0:T(8,128)(2,1)} %bitcast.24), channel_id=1, source_target_pairs={{1,0},{2,1},{3,2},{0,3},{5,4},{6,5},{7,6},{4,7},{9,8},{10,9},{11,1... | collective-permute-start | bytes 196616 | tf_op jit(solution)/shard_map/ppermute | solution.py:86
  5.1 4.0 %collective-permute-start = (bf16[32,1024]{1,0:T(8,128)(2,1)}, bf16[32,1024]{1,0:T(8,128)(2,1)S(1)}, u32[]{:S(2)}, u32[]{:S(2)}) collective-permute-start(bf16[32,1024]{1,0:T(8,128)(2,1)} %bitcast.25), channel_id=1, source_target_pairs={{3,0},{0,1},{1,2},{2,3},{7,4},{4,5},{5,6},{6,7},{11,8},{8,9},{9,10... | collective-permute-start | bytes 196616 | tf_op jit(solution)/shard_map/ppermute | solution.py:86
  5.1 5.2 %collective-permute-start.1 = (bf16[32,1024]{1,0:T(8,128)(2,1)}, bf16[32,1024]{1,0:T(8,128)(2,1)S(1)}, u32[]{:S(2)}, u32[]{:S(2)}) collective-permute-start(bf16[32,1024]{1,0:T(8,128)(2,1)} %bitcast.26), channel_id=1, source_target_pairs={{2,0},{3,1},{0,2},{1,3},{6,4},{7,5},{4,6},{5,7},{10,8},{11,9},{8,1... | collective-permute-start | bytes 196616 | tf_op jit(solution)/shard_map/ppermute | solution.py:86
  7.3 3.6 %collective-permute-start.2 = (bf16[32,1024]{1,0:T(8,128)(2,1)}, bf16[32,1024]{1,0:T(8,128)(2,1)S(1)}, u32[]{:S(2)}, u32[]{:S(2)}) collective-permute-start(bf16[32,1024]{1,0:T(8,128)(2,1)} %bitcast.27), channel_id=1, source_target_pairs={{1,0},{2,1},{3,2},{0,3},{5,4},{6,5},{7,6},{4,7},{9,8},{10,9},{11,1... | collective-permute-start | bytes 196616 | tf_op jit(solution)/shard_map/ppermute | solution.py:86
  10.9 2.2 %copy-start = (bf16[1,128,16384]{2,1,0:T(8,128)(2,1)S(1)}, bf16[1,128,16384]{2,1,0:T(8,128)(2,1)}, u32[]{:S(2)}) copy-start(bf16[1,128,16384]{2,1,0:T(8,128)(2,1)} %param.10) | copy-start | bytes 12582916
  13.1 0.7 %copy-start.1 = (f32[1,1024]{1,0:T(1,128)S(1)}, f32[1,1024]{1,0:T(1,128)}, u32[]{:S(2)}) copy-start(f32[1,1024]{1,0:T(1,128)} %scale_ref.1) | copy-start | bytes 12292
  13.8 43.8 %copy-start.4 = (bf16[1,32,1024]{2,1,0:T(8,128)(2,1)S(1)}, bf16[1,32,1024]{2,1,0:T(8,128)(2,1)}, u32[]{:S(2)}) copy-start(bf16[1,32,1024]{2,1,0:T(8,128)(2,1)} %param.9) | copy-start | bytes 196612
  13.8 43.9 %copy-start.2 = (bf16[1,32,1024]{2,1,0:T(8,128)(2,1)S(1)}, bf16[1,32,1024]{2,1,0:T(8,128)(2,1)}, u32[]{:S(2)}) copy-start(bf16[1,32,1024]{2,1,0:T(8,128)(2,1)} %param.8) | copy-start | bytes 196612
  13.8 46.4 %copy-start.3 = (bf16[1,32,1024]{2,1,0:T(8,128)(2,1)S(1)}, bf16[1,32,1024]{2,1,0:T(8,128)(2,1)}, u32[]{:S(2)}) copy-start(bf16[1,32,1024]{2,1,0:T(8,128)(2,1)} %param.7) | copy-start | bytes 196612
  51.4 4.5 %collective-permute-start.10 = (bf16[32,1024]{1,0:T(8,128)(2,1)S(1)}, bf16[32,1024]{1,0:T(8,128)(2,1)S(1)}, u32[]{:S(2)}, u32[]{:S(2)}) collective-permute-start(bf16[32,1024]{1,0:T(8,128)(2,1)S(1)} %get-tuple-element.8), channel_id=1, source_target_pairs={{3,0},{0,1},{1,2},{2,3},{7,4},{4,5},{5,6},{6,7},{11,8},{8,9},{9,10... | collective-permute-start | bytes 196616 | tf_op jit(solution)/shard_map/ppermute | solution.py:86
  53.3 4.3 %collective-permute-start.11 = (bf16[32,1024]{1,0:T(8,128)(2,1)S(1)}, bf16[32,1024]{1,0:T(8,128)(2,1)S(1)}, u32[]{:S(2)}, u32[]{:S(2)}) collective-permute-start(bf16[32,1024]{1,0:T(8,128)(2,1)S(1)} %get-tuple-element.10), channel_id=1, source_target_pairs={{2,0},{3,1},{0,2},{1,3},{6,4},{7,5},{4,6},{5,7},{10,8},{11,9},{8,1... | collective-permute-start | bytes 196616 | tf_op jit(solution)/shard_map/ppermute | solution.py:86
  53.6 4.0 %collective-permute-start.12 = (bf16[32,1024]{1,0:T(8,128)(2,1)S(1)}, bf16[32,1024]{1,0:T(8,128)(2,1)S(1)}, u32[]{:S(2)}, u32[]{:S(2)}) collective-permute-start(bf16[32,1024]{1,0:T(8,128)(2,1)S(1)} %get-tuple-element.9), channel_id=1, source_target_pairs={{1,0},{2,1},{3,2},{0,3},{5,4},{6,5},{7,6},{4,7},{9,8},{10,9},{11,1... | collective-permute-start | bytes 196616 | tf_op jit(solution)/shard_map/ppermute | solution.py:86
  54.7 4.7 %collective-permute-start.6 = (bf16[32,1024]{1,0:T(8,128)(2,1)S(1)}, bf16[32,1024]{1,0:T(8,128)(2,1)S(1)}, u32[]{:S(2)}, u32[]{:S(2)}) collective-permute-start(bf16[32,1024]{1,0:T(8,128)(2,1)S(1)} %get-tuple-element.11), channel_id=1, source_target_pairs={{3,0},{0,1},{1,2},{2,3},{7,4},{4,5},{5,6},{6,7},{11,8},{8,9},{9,10... | collective-permute-start | bytes 196616 | tf_op jit(solution)/shard_map/ppermute | solution.py:86
  54.8 5.3 %collective-permute-start.7 = (bf16[32,1024]{1,0:T(8,128)(2,1)S(1)}, bf16[32,1024]{1,0:T(8,128)(2,1)S(1)}, u32[]{:S(2)}, u32[]{:S(2)}) collective-permute-start(bf16[32,1024]{1,0:T(8,128)(2,1)S(1)} %get-tuple-element.13), channel_id=1, source_target_pairs={{2,0},{3,1},{0,2},{1,3},{6,4},{7,5},{4,6},{5,7},{10,8},{11,9},{8,1... | collective-permute-start | bytes 196616 | tf_op jit(solution)/shard_map/ppermute | solution.py:86
  55.9 4.2 %collective-permute-start.8 = (bf16[32,1024]{1,0:T(8,128)(2,1)S(1)}, bf16[32,1024]{1,0:T(8,128)(2,1)S(1)}, u32[]{:S(2)}, u32[]{:S(2)}) collective-permute-start(bf16[32,1024]{1,0:T(8,128)(2,1)S(1)} %get-tuple-element.12), channel_id=1, source_target_pairs={{1,0},{2,1},{3,2},{0,3},{5,4},{6,5},{7,6},{4,7},{9,8},{10,9},{11,1... | collective-permute-start | bytes 196616 | tf_op jit(solution)/shard_map/ppermute | solution.py:86
  57.9 4.7 %collective-permute-start.13 = (bf16[32,1024]{1,0:T(8,128)(2,1)S(1)}, bf16[32,1024]{1,0:T(8,128)(2,1)S(1)}, u32[]{:S(2)}, u32[]{:S(2)}) collective-permute-start(bf16[32,1024]{1,0:T(8,128)(2,1)S(1)} %fusion.5), channel_id=1, source_target_pairs={{4,0},{0,4},{5,1},{1,5},{6,2},{2,6},{7,3},{3,7},{12,8},{8,12},{13,... | collective-permute-start | bytes 196616 | tf_op jit(solution)/shard_map/ppermute | solution.py:86
  60.2 4.8 %collective-permute-start.9 = (bf16[32,1024]{1,0:T(8,128)(2,1)S(1)}, bf16[32,1024]{1,0:T(8,128)(2,1)S(1)}, u32[]{:S(2)}, u32[]{:S(2)}) collective-permute-start(bf16[32,1024]{1,0:T(8,128)(2,1)S(1)} %add_convert_fusion), channel_id=1, source_target_pairs={{4,0},{0,4},{5,1},{1,5},{6,2},{2,6},{7,3},{3,7},{12,8},{8,12},{13,... | collective-permute-start | bytes 196616 | tf_op jit(solution)/shard_map/ppermute | solution.py:86

commit v2 on v1

v2 whole, which is shorter than its diff:
```python
import functools

import jax
import jax.numpy as jnp
from jax import lax
from jax.experimental import pallas as pl
from jax.experimental.pallas import tpu as pltpu
from jax.sharding import PartitionSpec as P

EPS = 1e-06
F32 = jnp.float32
BF16 = jnp.bfloat16


def tile_of(extent, limit):
    size = limit
    while size > 128 and extent % size:
        size //= 2
    return size if extent % size == 0 else extent


def section_kernel(tiles, rows, parts, outs, me_ref, *refs):
    blocks, refs = refs[:parts], refs[parts:]
    scale_ref, s_ref, wi_ref, wo_ref = refs[:4]
    out_refs, refs = refs[4 : 4 + outs], refs[4 + outs :]
    n_ref, g_ref, af, ab, wit, wot = refs
    step = pl.program_id(0)
    me = me_ref[0]

    def place(k):
        return pl.ds(pl.multiple_of((me ^ k) * rows, rows), rows)

    @pl.when(step == 0)
    def _():
        for k, block in enumerate(blocks):
            xf = block[0].astype(F32)
            r = lax.rsqrt(jnp.mean(xf * xf, axis=-1, keepdims=True) + EPS)
            n_ref[place(k), :] = (xf * r * scale_ref[...]).astype(BF16)
            g_ref[place(k), :] = block[1]
        af[...] = jnp.zeros_like(af)
        ab[...] = jnp.zeros_like(ab)

    wot[...] = wo_ref[...].T
    h = jnp.maximum(jnp.dot(n_ref[...], wi_ref[...], preferred_element_type=F32), 0.0).astype(BF16)
    af[...] += jnp.dot(h, wo_ref[...], preferred_element_type=F32)
    p = jnp.dot(g_ref[...], wot[...], preferred_element_type=F32)
    hg = jnp.where(s_ref[...] > 0, p, 0.0).astype(BF16)
    wit[...] = wi_ref[...].T
    ab[...] += jnp.dot(hg, wit[...], preferred_element_type=F32)

    @pl.when(step == tiles - 1)
    def _():
        for k in range(parts):
            out = out_refs[k % outs]
            out[k // outs, 0] = af[place(k), :].astype(BF16)
            out[k // outs, 1] = (ab[place(k), :] * scale_ref[...]).astype(BF16)


def section(me, blocks, scale, saved, w_in, w_out):
    parts = len(blocks)
    _, rows, width = blocks[0].shape
    tokens = parts * rows
    hidden = w_in.shape[1]
    tile = tile_of(hidden, 2048)
    tiles = hidden // tile
    outs = min(parts, 2)
    per = parts // outs
    block = pl.BlockSpec((2, rows, width), lambda i, me: (0, 0, 0))
    out = jax.ShapeDtypeStruct((per, 2, rows, width), BF16)
    return pl.pallas_call(
        functools.partial(section_kernel, tiles, rows, parts, outs),
        grid_spec=pltpu.PrefetchScalarGridSpec(
            num_scalar_prefetch=1,
            grid=(tiles,),
            in_specs=[block] * parts
            + [
                pl.BlockSpec((1, width), lambda i, me: (0, 0)),
                pl.BlockSpec((tokens, tile), lambda i, me: (0, i)),
                pl.BlockSpec((width, tile), lambda i, me: (0, i)),
                pl.BlockSpec((tile, width), lambda i, me: (i, 0)),
            ],
            out_specs=[pl.BlockSpec((per, 2, rows, width), lambda i, me: (0, 0, 0, 0))] * outs,
            scratch_shapes=[
                pltpu.VMEM((tokens, width), BF16),
                pltpu.VMEM((tokens, width), BF16),
                pltpu.VMEM((tokens, width), F32),
                pltpu.VMEM((tokens, width), F32),
                pltpu.VMEM((tile, width), BF16),
                pltpu.VMEM((width, tile), BF16),
            ],
        ),
        out_shape=[out] * outs,
        compiler_params=pltpu.CompilerParams(
            dimension_semantics=("arbitrary",), vmem_limit_bytes=52 << 20
        ),
        cost_estimate=pl.CostEstimate(
            flops=8 * tokens * width * hidden,
            bytes_accessed=4 * width * hidden + 2 * tokens * hidden,
            transcendentals=0,
        ),
        name="section",
    )(me, *blocks, scale, saved, w_in, w_out)


def sent(block, pipe_step, mp_xor):
    pipes, size = lax.axis_size("pipe"), lax.axis_size("mp")
    route = [
        (p * size + m, ((p + pipe_step) % pipes) * size + (m ^ mp_xor))
        for p in range(pipes)
        for m in range(size)
    ]
    return lax.ppermute(block, ("pipe", "mp"), route)


def onward(pair):
    return moved(pair, 0)


def moved(pair, mp_xor):
    if lax.axis_size("pipe") <= 2:
        return sent(pair, 1, mp_xor)
    return jnp.concatenate([sent(pair[:1], 1, mp_xor), sent(pair[1:], -1, mp_xor)])


def exchanged(own, size):
    blocks = {0: own}
    bit = size // 2
    while bit:
        for k in list(blocks):
            blocks[k ^ bit] = sent(blocks[k], 0, bit)
        bit //= 2
    return [blocks[k] for k in range(size)]


def rows_onward(x, g, u):
    if lax.axis_size("pipe") <= 2:
        return sent(jnp.stack([x, g, u]), 1, 0)
    return jnp.concatenate([sent(x[None], 1, 0), sent(jnp.stack([g, u]), -1, 0)])


def on_device(fwd_in, grad_in, saved_in, saved_hidden, gain, w_in, w_out):
    scale = gain[0][None, :]
    x, g, u = fwd_in[0], grad_in[0], saved_in[0]
    shifted = rows_onward(x, g, u)
    size = lax.axis_size("mp")
    rows = x.shape[0]
    own = jnp.stack([x, g])
    weights = (scale, saved_hidden[0], w_in[0], w_out[0])
    if size & (size - 1) == 0 and size > 1 and rows % 16 == 0:
        me = jnp.full((1,), lax.axis_index("mp"), jnp.int32)
        keep, give = section(me, exchanged(own, size), *weights)
        got = sent(give, 0, 1)
        total = jnp.zeros((2,) + x.shape, F32)
        for k in range(size // 2):
            pair = (keep[k].astype(F32) + got[k].astype(F32)).astype(BF16)
            total = total + moved(pair, 2 * k).astype(F32)
    else:
        whole = lax.all_gather(own, "mp", axis=1, tiled=True)
        (part,) = section(jnp.zeros((1,), jnp.int32), [whole], *weights)
        total = onward(lax.psum_scatter(part[0], "mp", scatter_dimension=1, tiled=True)).astype(F32)
    x, g, u = shifted
    section_out = (x.astype(F32) + total[0]).astype(BF16)
    uf = u.astype(F32)
    recip = lax.rsqrt(jnp.mean(uf * uf, axis=-1, keepdims=True) + EPS)
    scaled = total[1]
    inner = jnp.mean(scaled * uf, axis=-1, keepdims=True)
    input_grad = (g.astype(F32) + recip * scaled - uf * recip * recip * recip * inner).astype(BF16)
    return (section_out[None], input_grad[None])


def solution(mesh):
    rows = P("pipe", ("dp", "mp"), None)
    in_specs = (
        rows,
        rows,
        rows,
        P("pipe", "dp", "mp"),
        P("pipe", None),
        P("pipe", None, "mp"),
        P("pipe", "mp", None),
    )
    return jax.shard_map(
        on_device, mesh=mesh, in_specs=in_specs, out_specs=(rows, rows), check_vma=False
    )
```

time: 66.6 us -> 54.4 us (0.82)
  Pallas kernels: 37.6 us -> 28.1 us
  waiting for transfers between devices: 6.75 us -> 14 us
  starting transfers between devices: 14.8 us -> 8.04 us
  local copies, waits for them, and re-layouts: 5.98 us -> 2.39 us
    pallas_call x1, Pallas kernels: 37.6 us -> 28.1 us  [section(): pl.pallas_call(functools.partial(section_kernel, tiles, rows, parts, outs...]
    ppermute x14 -> x7, waiting for transfers between devices: 6.75 us -> 14 us  [sent(): return lax.ppermute(block, ('pipe', 'mp'), route)]
    ppermute x14 -> x7, starting transfers between devices: 14.8 us -> 8.04 us  [sent(): return lax.ppermute(block, ('pipe', 'mp'), route)]
    unnamed x12 -> x9, local copies, waits for them, and re-layouts: 4.14 us -> 1.54 us
    dynamic_update_slice x8 -> x0, local copies, waits for them, and re-layouts: 1.76 us -> none  [the longest x2 1.7 us: gathered(): full = lax.dynamic_update_slice(full, block, (me * rows, 0))]
    another operation x2 -> x1, local copies, waits for them, and re-layouts: 0.04 us -> 0.84 us  [on_device(): own = jnp.stack([x, g])]
  transfers between devices with their start and end apart: 14 -> 7, of which waited for: 7 -> 5; matrix products, arithmetic and copies ran while one was open for 3% -> 0% of each run, Pallas kernels for 0% -> 0%
where the time goes in v2:
time: 54.4 us; the launch traced here: 54.2 us
  Pallas kernels  28.1 us (52%)
  waiting for transfers between devices  14 us (26%)
  starting transfers between devices  8.04 us (15%)
  local copies, waits for them, and re-layouts  2.39 us (4%)
  other arithmetic  1 us (2%)
  between operations  0.67 us (1%)
    pallas_call x1, Pallas kernels, section(): pl.pallas_call(functools.partial(section_kernel, tiles, rows, parts, outs...  28.1 us
    ppermute x7, waiting for transfers between devices, sent(): return lax.ppermute(block, ('pipe', 'mp'), route)  14 us
    ppermute x7, starting transfers between devices, sent(): return lax.ppermute(block, ('pipe', 'mp'), route)  8.04 us
    unnamed x9, local copies, waits for them, and re-layouts  1.54 us
  transfers between devices with their start and end apart: 7, of which 5 were waited for; matrix products, arithmetic and copies ran while one was open for 0% of the time, Pallas kernels for 0%

profile of v2, /device:TPU:0, one launch (start us, length us, event | category | flops | bytes accessed | tf_op | source)
XLA Modules:
  0.0 54.2 jit_solution(5630184457855383824)
XLA Ops:
  0.6 0.8 %constant_dynamic-update-slice_fusion.1 = bf16[2,32,1024]{2,1,0:T(8,128)(2,1)S(1)} fusion(bf16[1,32,1024]{2,1,0:T(8,128)(2,1)} %param.7), kind=kLoop, calls=%fused_computation.19 | loop fusion | bytes 131072
  1.5 0.8 %constant_dynamic-update-slice_fusion.refs_0_ = bf16[2,32,1024]{2,1,0:T(8,128)(2,1)S(1)} fusion(bf16[2,32,1024]{2,1,0:T(8,128)(2,1)S(1)} %constant_dynamic-update-slice_fusion.1, bf16[1,32,1024]{2,1,0:T(8,128)(2,1)} %param.8), kind=kLoop, calls=%fused_computation.18 | loop fusion | bytes 131072 | tf_op jit(solution)/shard_map/stack | solution.py:147
  2.3 3.0 %collective-permute-start.2 = (bf16[2,32,1024]{2,1,0:T(8,128)(2,1)S(1)}, bf16[2,32,1024]{2,1,0:T(8,128)(2,1)S(1)}, u32[]{:S(2)}, u32[]{:S(2)}) collective-permute-start(bf16[2,32,1024]{2,1,0:T(8,128)(2,1)S(1)} %constant_dynamic-update-slice_fusion.refs_0_), channel_id=1, source_target_pairs={{0,2},{1,3},{2,0},{3,1},{4,6},{5,7},{6,4},{7,5},{8,10},{9,11},{10,... | collective-permute-start | bytes 393224 | tf_op jit(solution)/shard_map/ppermute | solution.py:112
  5.3 0.0 collective-permute-start.1
  5.3 3.5 %collective-permute-done.2.refs_2_ = bf16[2,32,1024]{2,1,0:T(8,128)(2,1)S(1)} collective-permute-done((bf16[2,32,1024]{2,1,0:T(8,128)(2,1)S(1)}, bf16[2,32,1024]{2,1,0:T(8,128)(2,1)S(1)}, u32[]{:S(2)}, u32[]{:S(2)}) %collective-permute-start.2) | collective-permute-done | bytes 131104 | tf_op jit(solution)/shard_map/ppermute | solution.py:112
  8.8 0.0 collective-permute-start.3
  8.8 0.0 collective-permute-done.1.refs_1_
  8.8 1.3 %collective-permute-done.3.refs_3_ = bf16[2,32,1024]{2,1,0:T(8,128)(2,1)S(1)} collective-permute-done((bf16[2,32,1024]{2,1,0:T(8,128)(2,1)S(1)}, bf16[2,32,1024]{2,1,0:T(8,128)(2,1)S(1)}, u32[]{:S(2)}, u32[]{:S(2)}) %collective-permute-start.3) | collective-permute-done | bytes 131104 | tf_op jit(solution)/shard_map/ppermute | solution.py:112
  10.1 0.0 copy-start
  10.1 0.7 %copy-done = f32[1,1024]{1,0:T(1,128)S(1)} copy-done((f32[1,1024]{1,0:T(1,128)S(1)}, f32[1,1024]{1,0:T(1,128)}, u32[]{:S(2)}) %copy-start) | copy-done | bytes 4120
  10.8 0.0 copy-start.1
  10.8 0.0 copy-start.2
  10.8 0.0 copy-start.3
  10.8 28.1 %section.1 = (bf16[2,2,32,1024]{3,2,1,0:T(8,128)(2,1)S(1)}, bf16[2,2,32,1024]{3,2,1,0:T(8,128)(2,1)S(1)}) custom-call(s32[1]{0:T(128)} %bitcast.me_ref, bf16[2,32,1024]{2,1,0:T(8,128)(2,1)S(1)} %constant_dynamic-update-slice_fusion.refs_0_, bf16[2,32,1024]{2,1,0:T(8,128)(2,1)S(1)} %collective-permute-done.1.refs_1_, ...), custom_call_target="tpu_custom_call" | custom-call | flops 17179869184 | bytes 71303168 | tf_op jit(solution)/shard_map/section/pallas_call | solution.py:70
  38.9 0.2 collective-permute-start.4
  39.1 1.4 %collective-permute-done.4 = bf16[2,2,32,1024]{3,2,1,0:T(8,128)(2,1)S(1)} collective-permute-done((bf16[2,2,32,1024]{3,2,1,0:T(8,128)(2,1)S(1)}, bf16[2,2,32,1024]{3,2,1,0:T(8,128)(2,1)S(1)}, u32[]{:S(2)}, u32[]{:S(2)}) %collective-permute-start.4) | collective-permute-done | bytes 262176 | tf_op jit(solution)/shard_map/ppermute | solution.py:112
  40.5 0.1 fusion.7
  40.6 1.8 %collective-permute-start.5 = (bf16[2,32,1024]{2,1,0:T(8,128)(2,1)S(1)}, bf16[2,32,1024]{2,1,0:T(8,128)(2,1)S(1)}, u32[]{:S(2)}, u32[]{:S(2)}) collective-permute-start(bf16[2,32,1024]{2,1,0:T(8,128)(2,1)S(1)} %get-tuple-element.8), channel_id=1, source_target_pairs={{0,4},{1,5},{2,6},{3,7},{4,0},{5,1},{6,2},{7,3},{8,12},{9,13},{10,... | collective-permute-start | bytes 393224 | tf_op jit(solution)/shard_map/ppermute | solution.py:112
  42.4 1.4 %collective-permute-start.6 = (bf16[2,32,1024]{2,1,0:T(8,128)(2,1)S(1)}, bf16[2,32,1024]{2,1,0:T(8,128)(2,1)S(1)}, u32[]{:S(2)}, u32[]{:S(2)}) collective-permute-start(bf16[2,32,1024]{2,1,0:T(8,128)(2,1)S(1)} %get-tuple-element.9), channel_id=1, source_target_pairs={{0,6},{1,7},{2,4},{3,5},{4,2},{5,3},{6,0},{7,1},{8,14},{9,15},{10,... | collective-permute-start | bytes 393224 | tf_op jit(solution)/shard_map/ppermute | solution.py:112
  43.9 0.0 copy-done.1
  43.9 0.0 copy-done.2
  43.9 0.0 copy-done.3
  43.9 1.6 %collective-permute-start = (bf16[3,32,1024]{2,1,0:T(8,128)(2,1)S(1)}, bf16[3,32,1024]{2,1,0:T(8,128)(2,1)S(1)}, u32[]{:S(2)}, u32[]{:S(2)}) collective-permute-start(bf16[3,32,1024]{2,1,0:T(8,128)(2,1)S(1)} %pad_maximum_fusion), channel_id=1, source_target_pairs={{0,4},{1,5},{2,6},{3,7},{4,0},{5,1},{6,2},{7,3},{8,12},{9,13},{10,... | collective-permute-start | bytes 589832 | tf_op jit(solution)/shard_map/ppermute | solution.py:112
  45.5 3.9 %collective-permute-done.5 = bf16[2,32,1024]{2,1,0:T(8,128)(2,1)S(1)} collective-permute-done((bf16[2,32,1024]{2,1,0:T(8,128)(2,1)S(1)}, bf16[2,32,1024]{2,1,0:T(8,128)(2,1)S(1)}, u32[]{:S(2)}, u32[]{:S(2)}) %collective-permute-start.5) | collective-permute-done | bytes 131104 | tf_op jit(solution)/shard_map/ppermute | solution.py:112
  49.4 0.0 collective-permute-done.6
  49.4 3.8 %collective-permute-done = bf16[3,32,1024]{2,1,0:T(8,128)(2,1)S(1)} collective-permute-done((bf16[3,32,1024]{2,1,0:T(8,128)(2,1)S(1)}, bf16[3,32,1024]{2,1,0:T(8,128)(2,1)S(1)}, u32[]{:S(2)}, u32[]{:S(2)}) %collective-permute-start) | collective-permute-done | bytes 196640 | tf_op jit(solution)/shard_map/ppermute | solution.py:112
  53.3 0.1 fusion
  53.4 0.7 %fusion.5 = (bf16[1,32,1024]{2,1,0:T(8,128)(2,1)}, bf16[1,32,1024]{2,1,0:T(8,128)(2,1)}) fusion(f32[2,32,1024]{2,1,0:T(8,128)S(1)} %convert_add_fusion, bf16[3,32,1024]{2,1,0:T(8,128)(2,1)S(1)} %collective-permute-done, f32[32]{0:T(128)S(1)} %get-tuple-element.13, f32[32]{0:T(128)S(1)} %get-tuple-element.12), kind=kLoop, calls=%fused_computation.12 | loop fusion | flops 425984 | bytes 590080 | tf_op jit(solution)/shard_map/convert_element_type | solution.py:167
  (3 shorter events, 0.1 us)
Async XLA Ops:
  2.3 6.5 %collective-permute-start.2 = (bf16[2,32,1024]{2,1,0:T(8,128)(2,1)S(1)}, bf16[2,32,1024]{2,1,0:T(8,128)(2,1)S(1)}, u32[]{:S(2)}, u32[]{:S(2)}) collective-permute-start(bf16[2,32,1024]{2,1,0:T(8,128)(2,1)S(1)} %constant_dynamic-update-slice_fusion.refs_0_), channel_id=1, source_target_pairs={{0,2},{1,3},{2,0},{3,1},{4,6},{5,7},{6,4},{7,5},{8,10},{9,11},{10,... | collective-permute-start | bytes 393224 | tf_op jit(solution)/shard_map/ppermute | solution.py:112
  5.3 3.5 %collective-permute-start.1 = (bf16[2,32,1024]{2,1,0:T(8,128)(2,1)S(1)}, bf16[2,32,1024]{2,1,0:T(8,128)(2,1)S(1)}, u32[]{:S(2)}, u32[]{:S(2)}) collective-permute-start(bf16[2,32,1024]{2,1,0:T(8,128)(2,1)S(1)} %constant_dynamic-update-slice_fusion.refs_0_), channel_id=1, source_target_pairs={{0,1},{1,0},{2,3},{3,2},{4,5},{5,4},{6,7},{7,6},{8,9},{9,8},{10,11... | collective-permute-start | bytes 393224 | tf_op jit(solution)/shard_map/ppermute | solution.py:112
  8.8 1.3 %collective-permute-start.3 = (bf16[2,32,1024]{2,1,0:T(8,128)(2,1)S(1)}, bf16[2,32,1024]{2,1,0:T(8,128)(2,1)S(1)}, u32[]{:S(2)}, u32[]{:S(2)}) collective-permute-start(bf16[2,32,1024]{2,1,0:T(8,128)(2,1)S(1)} %collective-permute-done.2.refs_2_), channel_id=1, source_target_pairs={{0,1},{1,0},{2,3},{3,2},{4,5},{5,4},{6,7},{7,6},{8,9},{9,8},{10,11... | collective-permute-start | bytes 393224 | tf_op jit(solution)/shard_map/ppermute | solution.py:112
  10.1 0.7 %copy-start = (f32[1,1024]{1,0:T(1,128)S(1)}, f32[1,1024]{1,0:T(1,128)}, u32[]{:S(2)}) copy-start(f32[1,1024]{1,0:T(1,128)} %refs_4_.1) | copy-start | bytes 12292
  10.8 33.0 %copy-start.1 = (bf16[1,32,1024]{2,1,0:T(8,128)(2,1)S(1)}, bf16[1,32,1024]{2,1,0:T(8,128)(2,1)}, u32[]{:S(2)}) copy-start(bf16[1,32,1024]{2,1,0:T(8,128)(2,1)} %param.7) | copy-start | bytes 196612
  10.8 33.0 %copy-start.2 = (bf16[1,32,1024]{2,1,0:T(8,128)(2,1)S(1)}, bf16[1,32,1024]{2,1,0:T(8,128)(2,1)}, u32[]{:S(2)}) copy-start(bf16[1,32,1024]{2,1,0:T(8,128)(2,1)} %param.8) | copy-start | bytes 196612
  10.8 33.0 %copy-start.3 = (bf16[1,32,1024]{2,1,0:T(8,128)(2,1)S(1)}, bf16[1,32,1024]{2,1,0:T(8,128)(2,1)}, u32[]{:S(2)}) copy-start(bf16[1,32,1024]{2,1,0:T(8,128)(2,1)} %param.9) | copy-start | bytes 196612
  38.9 1.6 %collective-permute-start.4 = (bf16[2,2,32,1024]{3,2,1,0:T(8,128)(2,1)S(1)}, bf16[2,2,32,1024]{3,2,1,0:T(8,128)(2,1)S(1)}, u32[]{:S(2)}, u32[]{:S(2)}) collective-permute-start(bf16[2,2,32,1024]{3,2,1,0:T(8,128)(2,1)S(1)} %get-tuple-element.5), channel_id=1, source_target_pairs={{0,1},{1,0},{2,3},{3,2},{4,5},{5,4},{6,7},{7,6},{8,9},{9,8},{10,11... | collective-permute-start | bytes 786440 | tf_op jit(solution)/shard_map/ppermute | solution.py:112
  40.6 8.8 %collective-permute-start.5 = (bf16[2,32,1024]{2,1,0:T(8,128)(2,1)S(1)}, bf16[2,32,1024]{2,1,0:T(8,128)(2,1)S(1)}, u32[]{:S(2)}, u32[]{:S(2)}) collective-permute-start(bf16[2,32,1024]{2,1,0:T(8,128)(2,1)S(1)} %get-tuple-element.8), channel_id=1, source_target_pairs={{0,4},{1,5},{2,6},{3,7},{4,0},{5,1},{6,2},{7,3},{8,12},{9,13},{10,... | collective-permute-start | bytes 393224 | tf_op jit(solution)/shard_map/ppermute | solution.py:112
  42.4 7.0 %collective-permute-start.6 = (bf16[2,32,1024]{2,1,0:T(8,128)(2,1)S(1)}, bf16[2,32,1024]{2,1,0:T(8,128)(2,1)S(1)}, u32[]{:S(2)}, u32[]{:S(2)}) collective-permute-start(bf16[2,32,1024]{2,1,0:T(8,128)(2,1)S(1)} %get-tuple-element.9), channel_id=1, source_target_pairs={{0,6},{1,7},{2,4},{3,5},{4,2},{5,3},{6,0},{7,1},{8,14},{9,15},{10,... | collective-permute-start | bytes 393224 | tf_op jit(solution)/shard_map/ppermute | solution.py:112
  43.9 9.4 %collective-permute-start = (bf16[3,32,1024]{2,1,0:T(8,128)(2,1)S(1)}, bf16[3,32,1024]{2,1,0:T(8,128)(2,1)S(1)}, u32[]{:S(2)}, u32[]{:S(2)}) collective-permute-start(bf16[3,32,1024]{2,1,0:T(8,128)(2,1)S(1)} %pad_maximum_fusion), channel_id=1, source_target_pairs={{0,4},{1,5},{2,6},{3,7},{4,0},{5,1},{6,2},{7,3},{8,12},{9,13},{10,... | collective-permute-start | bytes 589832 | tf_op jit(solution)/shard_map/ppermute | solution.py:112

commit v3 on v2

v3 whole, which is shorter than its diff:
```python
import functools

import jax
import jax.numpy as jnp
from jax import lax
from jax.experimental import pallas as pl
from jax.experimental.pallas import tpu as pltpu
from jax.sharding import PartitionSpec as P

EPS = 1e-06
F32 = jnp.float32
BF16 = jnp.bfloat16


def tile_of(extent, limit):
    size = limit
    while size > 128 and extent % size:
        size //= 2
    return size if extent % size == 0 else extent


def pack_kernel(x_ref, g_ref, u_ref, gain_ref, own_ref, all_ref, scale_ref):
    x, g = x_ref[...], g_ref[...]
    xf = x.astype(F32)
    r = lax.rsqrt(jnp.mean(xf * xf, axis=-1, keepdims=True) + EPS)
    own_ref[0] = (xf * r * gain_ref[...]).astype(BF16)
    own_ref[1] = g
    all_ref[0] = x
    all_ref[1] = g
    all_ref[2] = u_ref[...]
    scale_ref[...] = gain_ref[...]


def packed(x, g, u, gain):
    return pl.pallas_call(
        pack_kernel,
        out_shape=[
            pltpu.VMEM((2,) + x.shape, BF16),
            pltpu.VMEM((3,) + x.shape, BF16),
            pltpu.VMEM(gain.shape, F32),
        ],
        name="pack",
    )(x, g, u, gain)


def tile_copies(tile, at, sources, targets, sems):
    wi, wo = sources
    cut = pl.ds(at * tile if isinstance(at, int) else pl.multiple_of(at * tile, tile), tile)
    return [
        pltpu.make_async_copy(wi.at[:, cut], targets[0], sems.at[0]),
        pltpu.make_async_copy(wo.at[cut, :], targets[1], sems.at[1]),
    ]


def load_kernel(tile, wi_hbm, wo_hbm, wi_ref, wo_ref, sems):
    copies = tile_copies(tile, 0, (wi_hbm, wo_hbm), (wi_ref, wo_ref), sems)
    for copy in copies:
        copy.start()
    for copy in copies:
        copy.wait()


def first_tile(tile, w_in, w_out):
    width = w_in.shape[0]
    return pl.pallas_call(
        functools.partial(load_kernel, tile),
        in_specs=[pl.BlockSpec(memory_space=pltpu.HBM)] * 2,
        out_specs=[pl.BlockSpec(memory_space=pltpu.VMEM)] * 2,
        out_shape=[pltpu.VMEM((width, tile), BF16), pltpu.VMEM((tile, width), BF16)],
        scratch_shapes=[pltpu.SemaphoreType.DMA((2,))],
        compiler_params=pltpu.CompilerParams(vmem_limit_bytes=24 << 20),
        cost_estimate=pl.CostEstimate(
            flops=0, bytes_accessed=8 * tile * width, transcendentals=0
        ),
        name="load",
    )(w_in, w_out)


def section_kernel(tiles, tile, rows, parts, outs, me_ref, *refs):
    blocks, refs = refs[:parts], refs[parts:]
    scale_ref, s_ref, refs = refs[0], refs[1], refs[2:]
    first, sources, refs = refs[:2], refs[2:4], refs[4:]
    out_refs, refs = refs[:outs], refs[outs:]
    n_ref, g_ref, af, ab, wit, wot, wi_buf, wo_buf, sems = refs
    step = pl.program_id(0)
    me = me_ref[0]

    def place(k):
        return pl.ds(pl.multiple_of((me ^ k) * rows, rows), rows)

    def fetch(at, slot):
        targets = (wi_buf.at[slot], wo_buf.at[slot])
        return tile_copies(tile, at, sources, targets, sems.at[slot])

    def compute(wi, wo):
        half = tile // 2
        low, high = slice(0, half), slice(half, tile)

        def hidden(cut):
            h = jnp.dot(n_ref[...], wi[:, cut], preferred_element_type=F32)
            return jnp.maximum(h, 0.0).astype(BF16)

        def hidden_grad(cut):
            p = jnp.dot(g_ref[...], wot[:, cut], preferred_element_type=F32)
            at = pl.multiple_of(step * tile + cut.start, half)
            return jnp.where(s_ref[:, pl.ds(at, half)] > 0, p, 0.0).astype(BF16)

        wot[:, low] = wo[low, :].T
        h = hidden(low)
        wit[low, :] = wi[:, low].T
        af[...] += jnp.dot(h, wo[low, :], preferred_element_type=F32)
        wot[:, high] = wo[high, :].T
        hg = hidden_grad(low)
        h = hidden(high)
        wit[high, :] = wi[:, high].T
        ab[...] += jnp.dot(hg, wit[low, :], preferred_element_type=F32)
        af[...] += jnp.dot(h, wo[high, :], preferred_element_type=F32)
        ab[...] += jnp.dot(hidden_grad(high), wit[high, :], preferred_element_type=F32)

    @pl.when(step == 0)
    def _():
        for at in range(1, min(3, tiles)):
            for copy in fetch(at, at % 2):
                copy.start()
        for k, block in enumerate(blocks):
            n_ref[place(k), :] = block[0]
            g_ref[place(k), :] = block[1]
        af[...] = jnp.zeros_like(af)
        ab[...] = jnp.zeros_like(ab)
        compute(*first)

    @pl.when(step > 0)
    def _():
        slot = lax.rem(step, 2)
        for copy in fetch(step, slot):
            copy.wait()
        compute(wi_buf.at[slot], wo_buf.at[slot])

        @pl.when(step + 2 < tiles)
        def _():
            for copy in fetch(step + 2, slot):
                copy.start()

    @pl.when(step == tiles - 1)
    def _():
        for k in range(parts):
            out = out_refs[k % outs]
            out[k // outs, 0] = af[place(k), :].astype(BF16)
            out[k // outs, 1] = (ab[place(k), :] * scale_ref[...]).astype(BF16)


def section(tile, me, blocks, scale, first, saved, w_in, w_out):
    parts = len(blocks)
    _, rows, width = blocks[0].shape
    tokens = parts * rows
    hidden = w_in.shape[1]
    tiles = hidden // tile
    outs = min(parts, 2)
    per = parts // outs
    inside = pl.BlockSpec(memory_space=pltpu.VMEM)
    outside = pl.BlockSpec(memory_space=pltpu.HBM)
    out = jax.ShapeDtypeStruct((per, 2, rows, width), BF16)
    return pl.pallas_call(
        functools.partial(section_kernel, tiles, tile, rows, parts, outs),
        grid_spec=pltpu.PrefetchScalarGridSpec(
            num_scalar_prefetch=1,
            grid=(tiles,),
            in_specs=[inside] * (parts + 4) + [outside] * 2,
            out_specs=[inside] * outs,
            scratch_shapes=[
                pltpu.VMEM((tokens, width), BF16),
                pltpu.VMEM((tokens, width), BF16),
                pltpu.VMEM((tokens, width), F32),
                pltpu.VMEM((tokens, width), F32),
                pltpu.VMEM((tile, width), BF16),
                pltpu.VMEM((width, tile), BF16),
                pltpu.VMEM((2, width, tile), BF16),
                pltpu.VMEM((2, tile, width), BF16),
                pltpu.SemaphoreType.DMA((2, 2)),
            ],
        ),
        out_shape=[out] * outs,
        compiler_params=pltpu.CompilerParams(
            dimension_semantics=("arbitrary",), vmem_limit_bytes=36 << 20
        ),
        cost_estimate=pl.CostEstimate(
            flops=8 * tokens * width * hidden,
            bytes_accessed=4 * width * hidden + 2 * tokens * hidden,
            transcendentals=0,
        ),
        name="section",
    )(me, *blocks, scale, saved, *first, w_in, w_out)


def sent(block, pipe_step, mp_xor):
    pipes, size = lax.axis_size("pipe"), lax.axis_size("mp")
    route = [
        (p * size + m, ((p + pipe_step) % pipes) * size + (m ^ mp_xor))
        for p in range(pipes)
        for m in range(size)
    ]
    return lax.ppermute(block, ("pipe", "mp"), route)


def onward(pair):
    return moved(pair, 0)


def moved(pair, mp_xor):
    if lax.axis_size("pipe") <= 2:
        return sent(pair, 1, mp_xor)
    return jnp.concatenate([sent(pair[:1], 1, mp_xor), sent(pair[1:], -1, mp_xor)])


def exchanged(own, size):
    blocks = {0: own}
    for k in sorted(range(1, size), key=lambda k: -k):
        blocks[k] = sent(own, 0, k)
    return [blocks[k] for k in range(size)]


def rows_onward(three):
    if lax.axis_size("pipe") <= 2:
        return sent(three, 1, 0)
    return jnp.concatenate([sent(three[:1], 1, 0), sent(three[1:], -1, 0)])


def on_device(fwd_in, grad_in, saved_in, saved_hidden, gain, w_in, w_out):
    own, three, scale = packed(fwd_in[0], grad_in[0], saved_in[0], gain[0][None, :])
    shifted = rows_onward(three)
    size = lax.axis_size("mp")
    rows = own.shape[1]
    arrays = (saved_hidden[0], w_in[0], w_out[0])
    tile = tile_of(w_in.shape[2], 2048)
    first = first_tile(tile, *arrays[1:])
    if size & (size - 1) == 0 and size > 1 and rows % 16 == 0:
        me = jnp.full((1,), lax.axis_index("mp"), jnp.int32)
        keep, give = section(tile, me, exchanged(own, size), scale, first, *arrays)
        got = sent(give, 0, 1)
        total = jnp.zeros((2,) + own.shape[1:], F32)
        for k in range(size // 2):
            pair = (keep[k].astype(F32) + got[k].astype(F32)).astype(BF16)
            total = total + moved(pair, 2 * k).astype(F32)
    else:
        whole = lax.all_gather(own, "mp", axis=1, tiled=True)
        me = jnp.zeros((1,), jnp.int32)
        (part,) = section(tile, me, [whole], scale, first, *arrays)
        total = onward(lax.psum_scatter(part[0], "mp", scatter_dimension=1, tiled=True)).astype(F32)
    x, g, u = shifted
    section_out = (x.astype(F32) + total[0]).astype(BF16)
    uf = u.astype(F32)
    recip = lax.rsqrt(jnp.mean(uf * uf, axis=-1, keepdims=True) + EPS)
    scaled = total[1]
    inner = jnp.mean(scaled * uf, axis=-1, keepdims=True)
    input_grad = (g.astype(F32) + recip * scaled - uf * recip * recip * recip * inner).astype(BF16)
    return (section_out[None], input_grad[None])


def solution(mesh):
    rows = P("pipe", ("dp", "mp"), None)
    in_specs = (
        rows,
        rows,
        rows,
        P("pipe", "dp", "mp"),
        P("pipe", None),
        P("pipe", None, "mp"),
        P("pipe", "mp", None),
    )
    return jax.shard_map(
        on_device, mesh=mesh, in_specs=in_specs, out_specs=(rows, rows), check_vma=False
    )
```

time: 54.4 us -> 53.2 us (0.978)
  Pallas kernels: 28.1 us -> 30.9 us
  local copies, waits for them, and re-layouts: 2.39 us -> 0.01 us
  waiting for transfers between devices: 14 us -> 11.9 us
    pallas_call x1 -> x3, Pallas kernels: 28.1 us -> 30.9 us  [the longest x1 26.3 us: section(): pl.pallas_call(functools.partial(section_kernel, tiles, tile, rows, parts...]
    ppermute x7, waiting for transfers between devices: 14 us -> 11.9 us  [sent(): return lax.ppermute(block, ('pipe', 'mp'), route)]
    unnamed x9 -> x2, local copies, waits for them, and re-layouts: 1.54 us -> 0.01 us
    another operation x1 -> x0, local copies, waits for them, and re-layouts: 0.84 us -> none  [on_device(): own = jnp.stack([x, g])]
  transfers between devices with their start and end apart: 7 -> 7, of which waited for: 5 -> 4; matrix products, arithmetic and copies ran while one was open for 0% -> 0% of each run, Pallas kernels for 0% -> 7%
where the time goes in v3:
time: 53.2 us; the launch traced here: 53.1 us
  Pallas kernels  30.9 us (58%)
  waiting for transfers between devices  11.9 us (22%)
  starting transfers between devices  8.56 us (16%)
  other arithmetic  0.98 us (2%)
  between operations  0.69 us (1%)
    pallas_call x1, Pallas kernels, section(): pl.pallas_call(functools.partial(section_kernel, tiles, tile, rows, parts...  26.3 us
    ppermute x7, waiting for transfers between devices, sent(): return lax.ppermute(block, ('pipe', 'mp'), route)  11.9 us
    ppermute x7, starting transfers between devices, sent(): return lax.ppermute(block, ('pipe', 'mp'), route)  8.56 us
    pallas_call x1, Pallas kernels, first_tile(): pl.pallas_call(functools.partial(load_kernel, tile), in_specs=[pl.BlockSp...  3.62 us
  transfers between devices with their start and end apart: 7, of which 4 were waited for; matrix products, arithmetic and copies ran while one was open for 0% of the time, Pallas kernels for 7%

profile of v3, /device:TPU:0, one launch (start us, length us, event | category | flops | bytes accessed | tf_op | source)
XLA Modules:
  0.0 53.1 jit_solution(3035269254126340740)
XLA Ops:
  0.6 1.0 %pack.1 = (bf16[2,32,1024]{2,1,0:T(8,128)(2,1)S(1)}, bf16[3,32,1024]{2,1,0:T(8,128)(2,1)S(1)}, f32[1,1024]{1,0:T(1,128)S(1)}) custom-call(bf16[32,1024]{1,0:T(8,128)(2,1)} %bitcast.16, bf16[32,1024]{1,0:T(8,128)(2,1)} %bitcast.17, bf16[32,1024]{1,0:T(8,128)(2,1)} %bitcast.18, f32[1,1024]{1,0:T(1,128)} %gain_ref.1), custom_call_target="tpu_custom_call" | custom-call | tf_op jit(solution)/shard_map/pack/pallas_call | solution.py:35
  1.7 2.5 %collective-permute-start.3 = (bf16[2,32,1024]{2,1,0:T(8,128)(2,1)S(1)}, bf16[2,32,1024]{2,1,0:T(8,128)(2,1)S(1)}, u32[]{:S(2)}, u32[]{:S(2)}) collective-permute-start(bf16[2,32,1024]{2,1,0:T(8,128)(2,1)S(1)} %get-tuple-element.10.refs_0_), channel_id=1, source_target_pairs={{0,3},{1,2},{2,1},{3,0},{4,7},{5,6},{6,5},{7,4},{8,11},{9,10},{10,... | collective-permute-start | bytes 393224 | tf_op jit(solution)/shard_map/ppermute | solution.py:202
  4.1 0.6 %collective-permute-start.2 = (bf16[2,32,1024]{2,1,0:T(8,128)(2,1)S(1)}, bf16[2,32,1024]{2,1,0:T(8,128)(2,1)S(1)}, u32[]{:S(2)}, u32[]{:S(2)}) collective-permute-start(bf16[2,32,1024]{2,1,0:T(8,128)(2,1)S(1)} %get-tuple-element.10.refs_0_), channel_id=1, source_target_pairs={{0,2},{1,3},{2,0},{3,1},{4,6},{5,7},{6,4},{7,5},{8,10},{9,11},{10,... | collective-permute-start | bytes 393224 | tf_op jit(solution)/shard_map/ppermute | solution.py:202
  4.8 0.0 collective-permute-start.1
  4.8 0.0 copy-start
  4.8 3.6 %load.1 = (bf16[1024,2048]{1,0:T(8,128)(2,1)S(1)}, bf16[2048,1024]{1,0:T(8,128)(2,1)S(1)}) custom-call(bf16[1024,16384]{1,0:T(8,128)(2,1)} %bitcast.12, bf16[16384,1024]{1,0:T(8,128)(2,1)} %bitcast.14), custom_call_target="tpu_custom_call" | custom-call | bytes 16777216 | tf_op jit(solution)/shard_map/load/pallas_call | solution.py:65
  8.4 0.0 collective-permute-done.3.refs_3_
  8.5 2.5 %collective-permute-done.2.refs_2_ = bf16[2,32,1024]{2,1,0:T(8,128)(2,1)S(1)} collective-permute-done((bf16[2,32,1024]{2,1,0:T(8,128)(2,1)S(1)}, bf16[2,32,1024]{2,1,0:T(8,128)(2,1)S(1)}, u32[]{:S(2)}, u32[]{:S(2)}) %collective-permute-start.2) | collective-permute-done | bytes 131104 | tf_op jit(solution)/shard_map/ppermute | solution.py:202
  11.0 0.0 collective-permute-done.1.refs_1_
  11.0 0.0 copy-done
  11.0 26.3 %section.1 = (bf16[2,2,32,1024]{3,2,1,0:T(8,128)(2,1)S(1)}, bf16[2,2,32,1024]{3,2,1,0:T(8,128)(2,1)S(1)}) custom-call(s32[1]{0:T(128)} %bitcast.3.me_ref, bf16[2,32,1024]{2,1,0:T(8,128)(2,1)S(1)} %get-tuple-element.10.refs_0_, bf16[2,32,1024]{2,1,0:T(8,128)(2,1)S(1)} %collective-permute-done.1.refs_1_, ...), custom_call_target="tpu_custom_call" | custom-call | flops 17179869184 | bytes 71303168 | tf_op jit(solution)/shard_map/section/pallas_call | solution.py:163
  37.3 0.1 collective-permute-start.4
  37.4 1.5 %collective-permute-done.4 = bf16[2,2,32,1024]{3,2,1,0:T(8,128)(2,1)S(1)} collective-permute-done((bf16[2,2,32,1024]{3,2,1,0:T(8,128)(2,1)S(1)}, bf16[2,2,32,1024]{3,2,1,0:T(8,128)(2,1)S(1)}, u32[]{:S(2)}, u32[]{:S(2)}) %collective-permute-start.4) | collective-permute-done | bytes 262176 | tf_op jit(solution)/shard_map/ppermute | solution.py:202
  38.9 0.1 fusion.7
  39.0 2.4 %collective-permute-start.5 = (bf16[2,32,1024]{2,1,0:T(8,128)(2,1)S(1)}, bf16[2,32,1024]{2,1,0:T(8,128)(2,1)S(1)}, u32[]{:S(2)}, u32[]{:S(2)}) collective-permute-start(bf16[2,32,1024]{2,1,0:T(8,128)(2,1)S(1)} %get-tuple-element.18), channel_id=1, source_target_pairs={{0,4},{1,5},{2,6},{3,7},{4,0},{5,1},{6,2},{7,3},{8,12},{9,13},{10,... | collective-permute-start | bytes 393224 | tf_op jit(solution)/shard_map/ppermute | solution.py:202
  41.4 1.4 %collective-permute-start.6 = (bf16[2,32,1024]{2,1,0:T(8,128)(2,1)S(1)}, bf16[2,32,1024]{2,1,0:T(8,128)(2,1)S(1)}, u32[]{:S(2)}, u32[]{:S(2)}) collective-permute-start(bf16[2,32,1024]{2,1,0:T(8,128)(2,1)S(1)} %get-tuple-element.19), channel_id=1, source_target_pairs={{0,6},{1,7},{2,4},{3,5},{4,2},{5,3},{6,0},{7,1},{8,14},{9,15},{10,... | collective-permute-start | bytes 393224 | tf_op jit(solution)/shard_map/ppermute | solution.py:202
  42.8 1.5 %collective-permute-start = (bf16[3,32,1024]{2,1,0:T(8,128)(2,1)S(1)}, bf16[3,32,1024]{2,1,0:T(8,128)(2,1)S(1)}, u32[]{:S(2)}, u32[]{:S(2)}) collective-permute-start(bf16[3,32,1024]{2,1,0:T(8,128)(2,1)S(1)} %get-tuple-element.9), channel_id=1, source_target_pairs={{0,4},{1,5},{2,6},{3,7},{4,0},{5,1},{6,2},{7,3},{8,12},{9,13},{10,... | collective-permute-start | bytes 589832 | tf_op jit(solution)/shard_map/ppermute | solution.py:202
  44.3 4.0 %collective-permute-done.5 = bf16[2,32,1024]{2,1,0:T(8,128)(2,1)S(1)} collective-permute-done((bf16[2,32,1024]{2,1,0:T(8,128)(2,1)S(1)}, bf16[2,32,1024]{2,1,0:T(8,128)(2,1)S(1)}, u32[]{:S(2)}, u32[]{:S(2)}) %collective-permute-start.5) | collective-permute-done | bytes 131104 | tf_op jit(solution)/shard_map/ppermute | solution.py:202
  48.3 0.0 collective-permute-done.6
  48.3 3.8 %collective-permute-done = bf16[3,32,1024]{2,1,0:T(8,128)(2,1)S(1)} collective-permute-done((bf16[3,32,1024]{2,1,0:T(8,128)(2,1)S(1)}, bf16[3,32,1024]{2,1,0:T(8,128)(2,1)S(1)}, u32[]{:S(2)}, u32[]{:S(2)}) %collective-permute-start) | collective-permute-done | bytes 196640 | tf_op jit(solution)/shard_map/ppermute | solution.py:202
  52.2 0.1 fusion
  52.3 0.7 %fusion.5 = (bf16[1,32,1024]{2,1,0:T(8,128)(2,1)}, bf16[1,32,1024]{2,1,0:T(8,128)(2,1)}) fusion(f32[2,32,1024]{2,1,0:T(8,128)S(1)} %convert_add_fusion, bf16[3,32,1024]{2,1,0:T(8,128)(2,1)S(1)} %collective-permute-done, f32[32]{0:T(128)S(1)} %get-tuple-element.23, f32[32]{0:T(128)S(1)} %get-tuple-element.22), kind=kLoop, calls=%fused_computation.11 | loop fusion | flops 425984 | bytes 590080 | tf_op jit(solution)/shard_map/convert_element_type | solution.py:255
  (2 shorter events, 0.0 us)
Async XLA Ops:
  1.7 6.8 %collective-permute-start.3 = (bf16[2,32,1024]{2,1,0:T(8,128)(2,1)S(1)}, bf16[2,32,1024]{2,1,0:T(8,128)(2,1)S(1)}, u32[]{:S(2)}, u32[]{:S(2)}) collective-permute-start(bf16[2,32,1024]{2,1,0:T(8,128)(2,1)S(1)} %get-tuple-element.10.refs_0_), channel_id=1, source_target_pairs={{0,3},{1,2},{2,1},{3,0},{4,7},{5,6},{6,5},{7,4},{8,11},{9,10},{10,... | collective-permute-start | bytes 393224 | tf_op jit(solution)/shard_map/ppermute | solution.py:202
  4.1 6.9 %collective-permute-start.2 = (bf16[2,32,1024]{2,1,0:T(8,128)(2,1)S(1)}, bf16[2,32,1024]{2,1,0:T(8,128)(2,1)S(1)}, u32[]{:S(2)}, u32[]{:S(2)}) collective-permute-start(bf16[2,32,1024]{2,1,0:T(8,128)(2,1)S(1)} %get-tuple-element.10.refs_0_), channel_id=1, source_target_pairs={{0,2},{1,3},{2,0},{3,1},{4,6},{5,7},{6,4},{7,5},{8,10},{9,11},{10,... | collective-permute-start | bytes 393224 | tf_op jit(solution)/shard_map/ppermute | solution.py:202
  4.8 6.2 %collective-permute-start.1 = (bf16[2,32,1024]{2,1,0:T(8,128)(2,1)S(1)}, bf16[2,32,1024]{2,1,0:T(8,128)(2,1)S(1)}, u32[]{:S(2)}, u32[]{:S(2)}) collective-permute-start(bf16[2,32,1024]{2,1,0:T(8,128)(2,1)S(1)} %get-tuple-element.10.refs_0_), channel_id=1, source_target_pairs={{0,1},{1,0},{2,3},{3,2},{4,5},{5,4},{6,7},{7,6},{8,9},{9,8},{10,11... | collective-permute-start | bytes 393224 | tf_op jit(solution)/shard_map/ppermute | solution.py:202
  4.8 6.2 %copy-start = (bf16[1,128,16384]{2,1,0:T(8,128)(2,1)S(1)}, bf16[1,128,16384]{2,1,0:T(8,128)(2,1)}, u32[]{:S(2)}) copy-start(bf16[1,128,16384]{2,1,0:T(8,128)(2,1)} %param.10) | copy-start | bytes 12582916
  37.3 1.6 %collective-permute-start.4 = (bf16[2,2,32,1024]{3,2,1,0:T(8,128)(2,1)S(1)}, bf16[2,2,32,1024]{3,2,1,0:T(8,128)(2,1)S(1)}, u32[]{:S(2)}, u32[]{:S(2)}) collective-permute-start(bf16[2,2,32,1024]{3,2,1,0:T(8,128)(2,1)S(1)} %get-tuple-element.15), channel_id=1, source_target_pairs={{0,1},{1,0},{2,3},{3,2},{4,5},{5,4},{6,7},{7,6},{8,9},{9,8},{10,11... | collective-permute-start | bytes 786440 | tf_op jit(solution)/shard_map/ppermute | solution.py:202
  39.0 9.3 %collective-permute-start.5 = (bf16[2,32,1024]{2,1,0:T(8,128)(2,1)S(1)}, bf16[2,32,1024]{2,1,0:T(8,128)(2,1)S(1)}, u32[]{:S(2)}, u32[]{:S(2)}) collective-permute-start(bf16[2,32,1024]{2,1,0:T(8,128)(2,1)S(1)} %get-tuple-element.18), channel_id=1, source_target_pairs={{0,4},{1,5},{2,6},{3,7},{4,0},{5,1},{6,2},{7,3},{8,12},{9,13},{10,... | collective-permute-start | bytes 393224 | tf_op jit(solution)/shard_map/ppermute | solution.py:202
  41.4 7.0 %collective-permute-start.6 = (bf16[2,32,1024]{2,1,0:T(8,128)(2,1)S(1)}, bf16[2,32,1024]{2,1,0:T(8,128)(2,1)S(1)}, u32[]{:S(2)}, u32[]{:S(2)}) collective-permute-start(bf16[2,32,1024]{2,1,0:T(8,128)(2,1)S(1)} %get-tuple-element.19), channel_id=1, source_target_pairs={{0,6},{1,7},{2,4},{3,5},{4,2},{5,3},{6,0},{7,1},{8,14},{9,15},{10,... | collective-permute-start | bytes 393224 | tf_op jit(solution)/shard_map/ppermute | solution.py:202
  42.8 9.4 %collective-permute-start = (bf16[3,32,1024]{2,1,0:T(8,128)(2,1)S(1)}, bf16[3,32,1024]{2,1,0:T(8,128)(2,1)S(1)}, u32[]{:S(2)}, u32[]{:S(2)}) collective-permute-start(bf16[3,32,1024]{2,1,0:T(8,128)(2,1)S(1)} %get-tuple-element.9), channel_id=1, source_target_pairs={{0,4},{1,5},{2,6},{3,7},{4,0},{5,1},{6,2},{7,3},{8,12},{9,13},{10,... | collective-permute-start | bytes 589832 | tf_op jit(solution)/shard_map/ppermute | solution.py:202

commit v4 on v3

--- a/solution.py
+++ b/solution.py
@@ -76,7 +76,7 @@
     )(w_in, w_out)
 
 
-def section_kernel(tiles, tile, rows, parts, outs, me_ref, *refs):
+def section_kernel(tiles, tile, depth, rows, parts, outs, me_ref, *refs):
     blocks, refs = refs[:parts], refs[parts:]
     scale_ref, s_ref, refs = refs[0], refs[1], refs[2:]
     first, sources, refs = refs[:2], refs[2:4], refs[4:]
@@ -119,8 +119,8 @@
 
     @pl.when(step == 0)
     def _():
-        for at in range(1, min(3, tiles)):
-            for copy in fetch(at, at % 2):
+        for at in range(1, min(depth + 1, tiles)):
+            for copy in fetch(at, at % depth):
                 copy.start()
         for k, block in enumerate(blocks):
             n_ref[place(k), :] = block[0]
@@ -131,14 +131,14 @@
 
     @pl.when(step > 0)
     def _():
-        slot = lax.rem(step, 2)
+        slot = lax.rem(step, depth)
         for copy in fetch(step, slot):
             copy.wait()
         compute(wi_buf.at[slot], wo_buf.at[slot])
 
-        @pl.when(step + 2 < tiles)
+        @pl.when(step + depth < tiles)
         def _():
-            for copy in fetch(step + 2, slot):
+            for copy in fetch(step + depth, slot):
                 copy.start()
 
     @pl.when(step == tiles - 1)
@@ -155,13 +155,14 @@
     tokens = parts * rows
     hidden = w_in.shape[1]
     tiles = hidden // tile
+    depth = 2
     outs = min(parts, 2)
     per = parts // outs
     inside = pl.BlockSpec(memory_space=pltpu.VMEM)
     outside = pl.BlockSpec(memory_space=pltpu.HBM)
     out = jax.ShapeDtypeStruct((per, 2, rows, width), BF16)
     return pl.pallas_call(
-        functools.partial(section_kernel, tiles, tile, rows, parts, outs),
+        functools.partial(section_kernel, tiles, tile, depth, rows, parts, outs),
         grid_spec=pltpu.PrefetchScalarGridSpec(
             num_scalar_prefetch=1,
             grid=(tiles,),
@@ -174,9 +175,9 @@
                 pltpu.VMEM((tokens, width), F32),
                 pltpu.VMEM((tile, width), BF16),
                 pltpu.VMEM((width, tile), BF16),
-                pltpu.VMEM((2, width, tile), BF16),
-                pltpu.VMEM((2, tile, width), BF16),
-                pltpu.SemaphoreType.DMA((2, 2)),
+                pltpu.VMEM((depth, width, tile), BF16),
+                pltpu.VMEM((depth, tile, width), BF16),
+                pltpu.SemaphoreType.DMA((depth, 2)),
             ],
         ),
         out_shape=[out] * outs,
@@ -214,8 +215,11 @@
 
 def exchanged(own, size):
     blocks = {0: own}
-    for k in sorted(range(1, size), key=lambda k: -k):
-        blocks[k] = sent(own, 0, k)
+    bit = size // 2
+    while bit:
+        for k in list(blocks):
+            blocks[k ^ bit] = sent(blocks[k], 0, bit)
+        bit //= 2
     return [blocks[k] for k in range(size)]
 
 

time: 53.2 us -> 54.9 us (1.032)
  local copies, waits for them, and re-layouts: 0.01 us -> 1 us
  waiting for transfers between devices: 11.9 us -> 12.7 us
    unnamed x2, local copies, waits for them, and re-layouts: 0.01 us -> 1 us
    ppermute x7, waiting for transfers between devices: 11.9 us -> 12.7 us  [sent(): return lax.ppermute(block, ('pipe', 'mp'), route)]
where the time goes in v4:
time: 54.9 us; the launch traced here: 54.7 us
  Pallas kernels  30.9 us (56%)
  waiting for transfers between devices  12.7 us (23%)
  starting transfers between devices  8.39 us (15%)
  local copies, waits for them, and re-layouts  1 us (2%)
  other arithmetic  0.98 us (2%)
  between operations  0.69 us (1%)
    pallas_call x1, Pallas kernels, section(): pl.pallas_call(functools.partial(section_kernel, tiles, tile, depth, rows...  26.3 us
    ppermute x7, waiting for transfers between devices, sent(): return lax.ppermute(block, ('pipe', 'mp'), route)  12.7 us
    ppermute x7, starting transfers between devices, sent(): return lax.ppermute(block, ('pipe', 'mp'), route)  8.39 us
    pallas_call x1, Pallas kernels, first_tile(): pl.pallas_call(functools.partial(load_kernel, tile), in_specs=[pl.BlockSp...  3.62 us
  transfers between devices with their start and end apart: 7, of which 4 were waited for; matrix products, arithmetic and copies ran while one was open for 0% of the time, Pallas kernels for 7%

profile of v4, /device:TPU:0, one launch (start us, length us, event | category | flops | bytes accessed | tf_op | source)
XLA Modules:
  0.0 54.7 jit_solution(18380464967874369205)
XLA Ops:
  0.6 1.0 %pack.1 = (bf16[2,32,1024]{2,1,0:T(8,128)(2,1)S(1)}, bf16[3,32,1024]{2,1,0:T(8,128)(2,1)S(1)}, f32[1,1024]{1,0:T(1,128)S(1)}) custom-call(bf16[32,1024]{1,0:T(8,128)(2,1)} %bitcast.16, bf16[32,1024]{1,0:T(8,128)(2,1)} %bitcast.17, bf16[32,1024]{1,0:T(8,128)(2,1)} %bitcast.18, f32[1,1024]{1,0:T(1,128)} %gain_ref.1), custom_call_target="tpu_custom_call" | custom-call | tf_op jit(solution)/shard_map/pack/pallas_call | solution.py:35
  1.7 3.0 %collective-permute-start.2 = (bf16[2,32,1024]{2,1,0:T(8,128)(2,1)S(1)}, bf16[2,32,1024]{2,1,0:T(8,128)(2,1)S(1)}, u32[]{:S(2)}, u32[]{:S(2)}) collective-permute-start(bf16[2,32,1024]{2,1,0:T(8,128)(2,1)S(1)} %get-tuple-element.10.refs_0_), channel_id=1, source_target_pairs={{0,2},{1,3},{2,0},{3,1},{4,6},{5,7},{6,4},{7,5},{8,10},{9,11},{10,... | collective-permute-start | bytes 393224 | tf_op jit(solution)/shard_map/ppermute | solution.py:203
  4.7 0.0 collective-permute-start.1
  4.7 3.5 %collective-permute-done.2.refs_2_ = bf16[2,32,1024]{2,1,0:T(8,128)(2,1)S(1)} collective-permute-done((bf16[2,32,1024]{2,1,0:T(8,128)(2,1)S(1)}, bf16[2,32,1024]{2,1,0:T(8,128)(2,1)S(1)}, u32[]{:S(2)}, u32[]{:S(2)}) %collective-permute-start.2) | collective-permute-done | bytes 131104 | tf_op jit(solution)/shard_map/ppermute | solution.py:203
  8.2 0.0 collective-permute-start.3
  8.2 0.0 copy-start
  8.2 3.6 %load.1 = (bf16[1024,2048]{1,0:T(8,128)(2,1)S(1)}, bf16[2048,1024]{1,0:T(8,128)(2,1)S(1)}) custom-call(bf16[1024,16384]{1,0:T(8,128)(2,1)} %bitcast.12, bf16[16384,1024]{1,0:T(8,128)(2,1)} %bitcast.14), custom_call_target="tpu_custom_call" | custom-call | bytes 16777216 | tf_op jit(solution)/shard_map/load/pallas_call | solution.py:65
  11.8 0.0 collective-permute-done.1.refs_1_
  11.8 0.0 collective-permute-done.3.refs_3_
  11.8 1.0 %copy-done = bf16[1,128,16384]{2,1,0:T(8,128)(2,1)S(1)} copy-done((bf16[1,128,16384]{2,1,0:T(8,128)(2,1)S(1)}, bf16[1,128,16384]{2,1,0:T(8,128)(2,1)}, u32[]{:S(2)}) %copy-start) | copy-done | bytes 4194328
  12.8 26.3 %section.1 = (bf16[2,2,32,1024]{3,2,1,0:T(8,128)(2,1)S(1)}, bf16[2,2,32,1024]{3,2,1,0:T(8,128)(2,1)S(1)}) custom-call(s32[1]{0:T(128)} %bitcast.3.me_ref, bf16[2,32,1024]{2,1,0:T(8,128)(2,1)S(1)} %get-tuple-element.10.refs_0_, bf16[2,32,1024]{2,1,0:T(8,128)(2,1)S(1)} %collective-permute-done.1.refs_1_, ...), custom_call_target="tpu_custom_call" | custom-call | flops 17179869184 | bytes 71303168 | tf_op jit(solution)/shard_map/section/pallas_call | solution.py:164
  39.1 0.6 %collective-permute-start.4 = (bf16[2,2,32,1024]{3,2,1,0:T(8,128)(2,1)S(1)}, bf16[2,2,32,1024]{3,2,1,0:T(8,128)(2,1)S(1)}, u32[]{:S(2)}, u32[]{:S(2)}) collective-permute-start(bf16[2,2,32,1024]{3,2,1,0:T(8,128)(2,1)S(1)} %get-tuple-element.15), channel_id=1, source_target_pairs={{0,1},{1,0},{2,3},{3,2},{4,5},{5,4},{6,7},{7,6},{8,9},{9,8},{10,11... | collective-permute-start | bytes 786440 | tf_op jit(solution)/shard_map/ppermute | solution.py:203
  39.7 1.2 %collective-permute-done.4 = bf16[2,2,32,1024]{3,2,1,0:T(8,128)(2,1)S(1)} collective-permute-done((bf16[2,2,32,1024]{3,2,1,0:T(8,128)(2,1)S(1)}, bf16[2,2,32,1024]{3,2,1,0:T(8,128)(2,1)S(1)}, u32[]{:S(2)}, u32[]{:S(2)}) %collective-permute-start.4) | collective-permute-done | bytes 262176 | tf_op jit(solution)/shard_map/ppermute | solution.py:203
  40.9 0.1 fusion.7
  40.9 1.8 %collective-permute-start.5 = (bf16[2,32,1024]{2,1,0:T(8,128)(2,1)S(1)}, bf16[2,32,1024]{2,1,0:T(8,128)(2,1)S(1)}, u32[]{:S(2)}, u32[]{:S(2)}) collective-permute-start(bf16[2,32,1024]{2,1,0:T(8,128)(2,1)S(1)} %get-tuple-element.18), channel_id=1, source_target_pairs={{0,4},{1,5},{2,6},{3,7},{4,0},{5,1},{6,2},{7,3},{8,12},{9,13},{10,... | collective-permute-start | bytes 393224 | tf_op jit(solution)/shard_map/ppermute | solution.py:203
  42.8 1.4 %collective-permute-start.6 = (bf16[2,32,1024]{2,1,0:T(8,128)(2,1)S(1)}, bf16[2,32,1024]{2,1,0:T(8,128)(2,1)S(1)}, u32[]{:S(2)}, u32[]{:S(2)}) collective-permute-start(bf16[2,32,1024]{2,1,0:T(8,128)(2,1)S(1)} %get-tuple-element.19), channel_id=1, source_target_pairs={{0,6},{1,7},{2,4},{3,5},{4,2},{5,3},{6,0},{7,1},{8,14},{9,15},{10,... | collective-permute-start | bytes 393224 | tf_op jit(solution)/shard_map/ppermute | solution.py:203
  44.2 1.5 %collective-permute-start = (bf16[3,32,1024]{2,1,0:T(8,128)(2,1)S(1)}, bf16[3,32,1024]{2,1,0:T(8,128)(2,1)S(1)}, u32[]{:S(2)}, u32[]{:S(2)}) collective-permute-start(bf16[3,32,1024]{2,1,0:T(8,128)(2,1)S(1)} %get-tuple-element.9), channel_id=1, source_target_pairs={{0,4},{1,5},{2,6},{3,7},{4,0},{5,1},{6,2},{7,3},{8,12},{9,13},{10,... | collective-permute-start | bytes 589832 | tf_op jit(solution)/shard_map/ppermute | solution.py:203
  45.7 4.2 %collective-permute-done.5 = bf16[2,32,1024]{2,1,0:T(8,128)(2,1)S(1)} collective-permute-done((bf16[2,32,1024]{2,1,0:T(8,128)(2,1)S(1)}, bf16[2,32,1024]{2,1,0:T(8,128)(2,1)S(1)}, u32[]{:S(2)}, u32[]{:S(2)}) %collective-permute-start.5) | collective-permute-done | bytes 131104 | tf_op jit(solution)/shard_map/ppermute | solution.py:203
  50.0 0.0 collective-permute-done.6
  50.0 3.8 %collective-permute-done = bf16[3,32,1024]{2,1,0:T(8,128)(2,1)S(1)} collective-permute-done((bf16[3,32,1024]{2,1,0:T(8,128)(2,1)S(1)}, bf16[3,32,1024]{2,1,0:T(8,128)(2,1)S(1)}, u32[]{:S(2)}, u32[]{:S(2)}) %collective-permute-start) | collective-permute-done | bytes 196640 | tf_op jit(solution)/shard_map/ppermute | solution.py:203
  53.8 0.1 fusion
  54.0 0.7 %fusion.5 = (bf16[1,32,1024]{2,1,0:T(8,128)(2,1)}, bf16[1,32,1024]{2,1,0:T(8,128)(2,1)}) fusion(f32[2,32,1024]{2,1,0:T(8,128)S(1)} %convert_add_fusion, bf16[3,32,1024]{2,1,0:T(8,128)(2,1)S(1)} %collective-permute-done, f32[32]{0:T(128)S(1)} %get-tuple-element.23, f32[32]{0:T(128)S(1)} %get-tuple-element.22), kind=kLoop, calls=%fused_computation.11 | loop fusion | flops 425984 | bytes 590080 | tf_op jit(solution)/shard_map/convert_element_type | solution.py:259
  (2 shorter events, 0.0 us)
Async XLA Ops:
  1.7 6.5 %collective-permute-start.2 = (bf16[2,32,1024]{2,1,0:T(8,128)(2,1)S(1)}, bf16[2,32,1024]{2,1,0:T(8,128)(2,1)S(1)}, u32[]{:S(2)}, u32[]{:S(2)}) collective-permute-start(bf16[2,32,1024]{2,1,0:T(8,128)(2,1)S(1)} %get-tuple-element.10.refs_0_), channel_id=1, source_target_pairs={{0,2},{1,3},{2,0},{3,1},{4,6},{5,7},{6,4},{7,5},{8,10},{9,11},{10,... | collective-permute-start | bytes 393224 | tf_op jit(solution)/shard_map/ppermute | solution.py:203
  4.7 7.1 %collective-permute-start.1 = (bf16[2,32,1024]{2,1,0:T(8,128)(2,1)S(1)}, bf16[2,32,1024]{2,1,0:T(8,128)(2,1)S(1)}, u32[]{:S(2)}, u32[]{:S(2)}) collective-permute-start(bf16[2,32,1024]{2,1,0:T(8,128)(2,1)S(1)} %get-tuple-element.10.refs_0_), channel_id=1, source_target_pairs={{0,1},{1,0},{2,3},{3,2},{4,5},{5,4},{6,7},{7,6},{8,9},{9,8},{10,11... | collective-permute-start | bytes 393224 | tf_op jit(solution)/shard_map/ppermute | solution.py:203
  8.2 3.7 %collective-permute-start.3 = (bf16[2,32,1024]{2,1,0:T(8,128)(2,1)S(1)}, bf16[2,32,1024]{2,1,0:T(8,128)(2,1)S(1)}, u32[]{:S(2)}, u32[]{:S(2)}) collective-permute-start(bf16[2,32,1024]{2,1,0:T(8,128)(2,1)S(1)} %collective-permute-done.2.refs_2_), channel_id=1, source_target_pairs={{0,1},{1,0},{2,3},{3,2},{4,5},{5,4},{6,7},{7,6},{8,9},{9,8},{10,11... | collective-permute-start | bytes 393224 | tf_op jit(solution)/shard_map/ppermute | solution.py:203
  8.2 4.7 %copy-start = (bf16[1,128,16384]{2,1,0:T(8,128)(2,1)S(1)}, bf16[1,128,16384]{2,1,0:T(8,128)(2,1)}, u32[]{:S(2)}) copy-start(bf16[1,128,16384]{2,1,0:T(8,128)(2,1)} %param.10) | copy-start | bytes 12582916
  39.1 1.7 %collective-permute-start.4 = (bf16[2,2,32,1024]{3,2,1,0:T(8,128)(2,1)S(1)}, bf16[2,2,32,1024]{3,2,1,0:T(8,128)(2,1)S(1)}, u32[]{:S(2)}, u32[]{:S(2)}) collective-permute-start(bf16[2,2,32,1024]{3,2,1,0:T(8,128)(2,1)S(1)} %get-tuple-element.15), channel_id=1, source_target_pairs={{0,1},{1,0},{2,3},{3,2},{4,5},{5,4},{6,7},{7,6},{8,9},{9,8},{10,11... | collective-permute-start | bytes 786440 | tf_op jit(solution)/shard_map/ppermute | solution.py:203
  40.9 9.0 %collective-permute-start.5 = (bf16[2,32,1024]{2,1,0:T(8,128)(2,1)S(1)}, bf16[2,32,1024]{2,1,0:T(8,128)(2,1)S(1)}, u32[]{:S(2)}, u32[]{:S(2)}) collective-permute-start(bf16[2,32,1024]{2,1,0:T(8,128)(2,1)S(1)} %get-tuple-element.18), channel_id=1, source_target_pairs={{0,4},{1,5},{2,6},{3,7},{4,0},{5,1},{6,2},{7,3},{8,12},{9,13},{10,... | collective-permute-start | bytes 393224 | tf_op jit(solution)/shard_map/ppermute | solution.py:203
  42.8 7.2 %collective-permute-start.6 = (bf16[2,32,1024]{2,1,0:T(8,128)(2,1)S(1)}, bf16[2,32,1024]{2,1,0:T(8,128)(2,1)S(1)}, u32[]{:S(2)}, u32[]{:S(2)}) collective-permute-start(bf16[2,32,1024]{2,1,0:T(8,128)(2,1)S(1)} %get-tuple-element.19), channel_id=1, source_target_pairs={{0,6},{1,7},{2,4},{3,5},{4,2},{5,3},{6,0},{7,1},{8,14},{9,15},{10,... | collective-permute-start | bytes 393224 | tf_op jit(solution)/shard_map/ppermute | solution.py:203
  44.2 9.6 %collective-permute-start = (bf16[3,32,1024]{2,1,0:T(8,128)(2,1)S(1)}, bf16[3,32,1024]{2,1,0:T(8,128)(2,1)S(1)}, u32[]{:S(2)}, u32[]{:S(2)}) collective-permute-start(bf16[3,32,1024]{2,1,0:T(8,128)(2,1)S(1)} %get-tuple-element.9), channel_id=1, source_target_pairs={{0,4},{1,5},{2,6},{3,7},{4,0},{5,1},{6,2},{7,3},{8,12},{9,13},{10,... | collective-permute-start | bytes 589832 | tf_op jit(solution)/shard_map/ppermute | solution.py:203

commit v5 on v4

--- a/solution.py
+++ b/solution.py
@@ -44,55 +44,57 @@
 
 
 def tile_copies(tile, at, sources, targets, sems):
-    wi, wo = sources
+    mask, wi, wo = sources
     cut = pl.ds(at * tile if isinstance(at, int) else pl.multiple_of(at * tile, tile), tile)
     return [
-        pltpu.make_async_copy(wi.at[:, cut], targets[0], sems.at[0]),
-        pltpu.make_async_copy(wo.at[cut, :], targets[1], sems.at[1]),
+        pltpu.make_async_copy(mask.at[:, cut], targets[0], sems.at[0]),
+        pltpu.make_async_copy(wi.at[:, cut], targets[1], sems.at[1]),
+        pltpu.make_async_copy(wo.at[cut, :], targets[2], sems.at[2]),
     ]
 
 
-def load_kernel(tile, wi_hbm, wo_hbm, wi_ref, wo_ref, sems):
-    copies = tile_copies(tile, 0, (wi_hbm, wo_hbm), (wi_ref, wo_ref), sems)
+def load_kernel(tile, *refs):
+    copies = tile_copies(tile, 0, refs[:3], refs[3:6], refs[6])
     for copy in copies:
         copy.start()
     for copy in copies:
         copy.wait()
 
 
-def first_tile(tile, w_in, w_out):
-    width = w_in.shape[0]
+def first_tile(tile, saved, w_in, w_out):
+    tokens, width = saved.shape[0], w_in.shape[0]
+    shapes = [(tokens, tile), (width, tile), (tile, width)]
     return pl.pallas_call(
         functools.partial(load_kernel, tile),
-        in_specs=[pl.BlockSpec(memory_space=pltpu.HBM)] * 2,
-        out_specs=[pl.BlockSpec(memory_space=pltpu.VMEM)] * 2,
-        out_shape=[pltpu.VMEM((width, tile), BF16), pltpu.VMEM((tile, width), BF16)],
-        scratch_shapes=[pltpu.SemaphoreType.DMA((2,))],
+        in_specs=[pl.BlockSpec(memory_space=pltpu.HBM)] * 3,
+        out_specs=[pl.BlockSpec(memory_space=pltpu.VMEM)] * 3,
+        out_shape=[pltpu.VMEM(shape, BF16) for shape in shapes],
+        scratch_shapes=[pltpu.SemaphoreType.DMA((3,))],
         compiler_params=pltpu.CompilerParams(vmem_limit_bytes=24 << 20),
         cost_estimate=pl.CostEstimate(
-            flops=0, bytes_accessed=8 * tile * width, transcendentals=0
+            flops=0, bytes_accessed=sum(4 * a * b for a, b in shapes), transcendentals=0
         ),
         name="load",
-    )(w_in, w_out)
-
-
-def section_kernel(tiles, tile, depth, rows, parts, outs, me_ref, *refs):
+    )(saved, w_in, w_out)
+
+
+def section_kernel(tiles, tile, depth, rows, parts, outs, *refs):
     blocks, refs = refs[:parts], refs[parts:]
-    scale_ref, s_ref, refs = refs[0], refs[1], refs[2:]
-    first, sources, refs = refs[:2], refs[2:4], refs[4:]
+    scale_ref, refs = refs[0], refs[1:]
+    first, sources, refs = refs[:3], refs[3:6], refs[6:]
     out_refs, refs = refs[:outs], refs[outs:]
-    n_ref, g_ref, af, ab, wit, wot, wi_buf, wo_buf, sems = refs
+    n_ref, g_ref, af, ab, wit, wot, s_buf, wi_buf, wo_buf, sems = refs
     step = pl.program_id(0)
-    me = me_ref[0]
+    me = lax.axis_index("mp") if parts > 1 else 0
 
     def place(k):
         return pl.ds(pl.multiple_of((me ^ k) * rows, rows), rows)
 
     def fetch(at, slot):
-        targets = (wi_buf.at[slot], wo_buf.at[slot])
+        targets = (s_buf.at[slot], wi_buf.at[slot], wo_buf.at[slot])
         return tile_copies(tile, at, sources, targets, sems.at[slot])
 
-    def compute(wi, wo):
+    def compute(mask, wi, wo):
         half = tile // 2
         low, high = slice(0, half), slice(half, tile)
 
@@ -102,8 +104,7 @@
 
         def hidden_grad(cut):
             p = jnp.dot(g_ref[...], wot[:, cut], preferred_element_type=F32)
-            at = pl.multiple_of(step * tile + cut.start, half)
-            return jnp.where(s_ref[:, pl.ds(at, half)] > 0, p, 0.0).astype(BF16)
+            return jnp.where(mask[:, cut] > 0, p, 0.0).astype(BF16)
 
         wot[:, low] = wo[low, :].T
         h = hidden(low)
@@ -134,7 +135,7 @@
         slot = lax.rem(step, depth)
         for copy in fetch(step, slot):
             copy.wait()
-        compute(wi_buf.at[slot], wo_buf.at[slot])
+        compute(s_buf.at[slot], wi_buf.at[slot], wo_buf.at[slot])
 
         @pl.when(step + depth < tiles)
         def _():
@@ -149,13 +150,13 @@
             out[k // outs, 1] = (ab[place(k), :] * scale_ref[...]).astype(BF16)
 
 
-def section(tile, me, blocks, scale, first, saved, w_in, w_out):
+def section(tile, blocks, scale, first, saved, w_in, w_out):
     parts = len(blocks)
     _, rows, width = blocks[0].shape
     tokens = parts * rows
     hidden = w_in.shape[1]
     tiles = hidden // tile
-    depth = 2
+    depth = 3
     outs = min(parts, 2)
     per = parts // outs
     inside = pl.BlockSpec(memory_space=pltpu.VMEM)
@@ -164,9 +165,9 @@
     return pl.pallas_call(
         functools.partial(section_kernel, tiles, tile, depth, rows, parts, outs),
         grid_spec=pltpu.PrefetchScalarGridSpec(
-            num_scalar_prefetch=1,
+            num_scalar_prefetch=0,
             grid=(tiles,),
-            in_specs=[inside] * (parts + 4) + [outside] * 2,
+            in_specs=[inside] * (parts + 4) + [outside] * 3,
             out_specs=[inside] * outs,
             scratch_shapes=[
                 pltpu.VMEM((tokens, width), BF16),
@@ -175,14 +176,15 @@
                 pltpu.VMEM((tokens, width), F32),
                 pltpu.VMEM((tile, width), BF16),
                 pltpu.VMEM((width, tile), BF16),
+                pltpu.VMEM((depth, tokens, tile), BF16),
                 pltpu.VMEM((depth, width, tile), BF16),
                 pltpu.VMEM((depth, tile, width), BF16),
-                pltpu.SemaphoreType.DMA((depth, 2)),
+                pltpu.SemaphoreType.DMA((depth, 3)),
             ],
         ),
         out_shape=[out] * outs,
         compiler_params=pltpu.CompilerParams(
-            dimension_semantics=("arbitrary",), vmem_limit_bytes=36 << 20
+            dimension_semantics=("arbitrary",), vmem_limit_bytes=42 << 20
         ),
         cost_estimate=pl.CostEstimate(
             flops=8 * tokens * width * hidden,
@@ -190,7 +192,7 @@
             transcendentals=0,
         ),
         name="section",
-    )(me, *blocks, scale, saved, *first, w_in, w_out)
+    )(*blocks, scale, *first, saved, w_in, w_out)
 
 
 def sent(block, pipe_step, mp_xor):
@@ -235,11 +237,12 @@
     size = lax.axis_size("mp")
     rows = own.shape[1]
     arrays = (saved_hidden[0], w_in[0], w_out[0])
+    arrays = [pltpu.with_memory_space_constraint(array, pltpu.HBM) for array in arrays]
     tile = tile_of(w_in.shape[2], 2048)
-    first = first_tile(tile, *arrays[1:])
+    first = first_tile(tile, *arrays)
+    first = [pltpu.with_memory_space_constraint(block, pltpu.VMEM) for block in first]
     if size & (size - 1) == 0 and size > 1 and rows % 16 == 0:
-        me = jnp.full((1,), lax.axis_index("mp"), jnp.int32)
-        keep, give = section(tile, me, exchanged(own, size), scale, first, *arrays)
+        keep, give = section(tile, exchanged(own, size), scale, first, *arrays)
         got = sent(give, 0, 1)
         total = jnp.zeros((2,) + own.shape[1:], F32)
         for k in range(size // 2):
@@ -247,8 +250,7 @@
             total = total + moved(pair, 2 * k).astype(F32)
     else:
         whole = lax.all_gather(own, "mp", axis=1, tiled=True)
-        me = jnp.zeros((1,), jnp.int32)
-        (part,) = section(tile, me, [whole], scale, first, *arrays)
+        (part,) = section(tile, [whole], scale, first, *arrays)
         total = onward(lax.psum_scatter(part[0], "mp", scatter_dimension=1, tiled=True)).astype(F32)
     x, g, u = shifted
     section_out = (x.astype(F32) + total[0]).astype(BF16)

time: 54.9 us -> 52.5 us (0.956)
  Pallas kernels: 30.9 us -> 29.5 us
  local copies, waits for them, and re-layouts: 1 us -> 0 us
    pallas_call x1, Pallas kernels: 26.3 us -> 24.8 us  [section(): pl.pallas_call(functools.partial(section_kernel, tiles, tile, depth, rows...]
    unnamed x2 -> x0, local copies, waits for them, and re-layouts: 1 us -> none
where the time goes in v5:
time: 52.5 us; the launch traced here: 52.3 us
  Pallas kernels  29.5 us (56%)
  waiting for transfers between devices  12.7 us (24%)
  starting transfers between devices  8.4 us (16%)
  other arithmetic  0.98 us (2%)
  between operations  0.69 us (1%)
    pallas_call x1, Pallas kernels, section(): pl.pallas_call(functools.partial(section_kernel, tiles, tile, depth, rows...  24.8 us
    ppermute x7, waiting for transfers between devices, sent(): return lax.ppermute(block, ('pipe', 'mp'), route)  12.7 us
    ppermute x7, starting transfers between devices, sent(): return lax.ppermute(block, ('pipe', 'mp'), route)  8.4 us
    pallas_call x1, Pallas kernels, first_tile(): pl.pallas_call(functools.partial(load_kernel, tile), in_specs=[pl.BlockSp...  3.67 us
  transfers between devices with their start and end apart: 7, of which 4 were waited for; matrix products, arithmetic and copies ran while one was open for 0% of the time, Pallas kernels for 7%

profile of v5, /device:TPU:0, one launch (start us, length us, event | category | flops | bytes accessed | tf_op | source)
XLA Modules:
  0.0 52.3 jit_solution(6361059482076422070)
XLA Ops:
  0.6 1.0 %pack.1 = (bf16[2,32,1024]{2,1,0:T(8,128)(2,1)S(1)}, bf16[3,32,1024]{2,1,0:T(8,128)(2,1)S(1)}, f32[1,1024]{1,0:T(1,128)S(1)}) custom-call(bf16[32,1024]{1,0:T(8,128)(2,1)} %bitcast.16, bf16[32,1024]{1,0:T(8,128)(2,1)} %bitcast.17, bf16[32,1024]{1,0:T(8,128)(2,1)} %bitcast.18, f32[1,1024]{1,0:T(1,128)} %gain_ref.1), custom_call_target="tpu_custom_call" | custom-call | tf_op jit(solution)/shard_map/pack/pallas_call | solution.py:35
  1.7 3.0 %collective-permute-start.2 = (bf16[2,32,1024]{2,1,0:T(8,128)(2,1)S(1)}, bf16[2,32,1024]{2,1,0:T(8,128)(2,1)S(1)}, u32[]{:S(2)}, u32[]{:S(2)}) collective-permute-start(bf16[2,32,1024]{2,1,0:T(8,128)(2,1)S(1)} %get-tuple-element.11.refs_0_), channel_id=1, source_target_pairs={{0,2},{1,3},{2,0},{3,1},{4,6},{5,7},{6,4},{7,5},{8,10},{9,11},{10,... | collective-permute-start | bytes 393224 | tf_op jit(solution)/shard_map/ppermute | solution.py:205
  4.7 0.0 collective-permute-start.1
  4.7 3.5 %collective-permute-done.2.refs_2_ = bf16[2,32,1024]{2,1,0:T(8,128)(2,1)S(1)} collective-permute-done((bf16[2,32,1024]{2,1,0:T(8,128)(2,1)S(1)}, bf16[2,32,1024]{2,1,0:T(8,128)(2,1)S(1)}, u32[]{:S(2)}, u32[]{:S(2)}) %collective-permute-start.2) | collective-permute-done | bytes 131104 | tf_op jit(solution)/shard_map/ppermute | solution.py:205
  8.2 0.0 collective-permute-start.3
  8.2 3.7 %load.1 = (bf16[128,2048]{1,0:T(8,128)(2,1)S(1)}, bf16[1024,2048]{1,0:T(8,128)(2,1)S(1)}, bf16[2048,1024]{1,0:T(8,128)(2,1)S(1)}) custom-call(bf16[128,16384]{1,0:T(8,128)(2,1)} %bitcast.14, bf16[1024,16384]{1,0:T(8,128)(2,1)} %bitcast.10, bf16[16384,1024]{1,0:T(8,128)(2,1)} %bitcast.12), custom_call_target="tpu_custom_call" | custom-call | bytes 17825792 | tf_op jit(solution)/shard_map/load/pallas_call | solution.py:67
  11.9 0.0 collective-permute-done.1.refs_1_
  11.9 0.0 collective-permute-done.3.refs_3_
  11.9 24.8 %section.1 = (bf16[2,2,32,1024]{3,2,1,0:T(8,128)(2,1)S(1)}, bf16[2,2,32,1024]{3,2,1,0:T(8,128)(2,1)S(1)}) custom-call(bf16[2,32,1024]{2,1,0:T(8,128)(2,1)S(1)} %get-tuple-element.11.refs_0_, bf16[2,32,1024]{2,1,0:T(8,128)(2,1)S(1)} %collective-permute-done.1.refs_1_, bf16[2,32,1024]{2,1,0:T(8,128)(2,1)S(1)} %collective-permute-done.2.refs_2_, ...), custom_call_target="tpu_custom_call" | custom-call | flops 17179869184 | bytes 71303168 | tf_op jit(solution)/shard_map/section/pallas_call | solution.py:165
  36.7 0.6 %collective-permute-start.4 = (bf16[2,2,32,1024]{3,2,1,0:T(8,128)(2,1)S(1)}, bf16[2,2,32,1024]{3,2,1,0:T(8,128)(2,1)S(1)}, u32[]{:S(2)}, u32[]{:S(2)}) collective-permute-start(bf16[2,2,32,1024]{3,2,1,0:T(8,128)(2,1)S(1)} %get-tuple-element.17), channel_id=1, source_target_pairs={{0,1},{1,0},{2,3},{3,2},{4,5},{5,4},{6,7},{7,6},{8,9},{9,8},{10,11... | collective-permute-start | bytes 786440 | tf_op jit(solution)/shard_map/ppermute | solution.py:205
  37.3 1.2 %collective-permute-done.4 = bf16[2,2,32,1024]{3,2,1,0:T(8,128)(2,1)S(1)} collective-permute-done((bf16[2,2,32,1024]{3,2,1,0:T(8,128)(2,1)S(1)}, bf16[2,2,32,1024]{3,2,1,0:T(8,128)(2,1)S(1)}, u32[]{:S(2)}, u32[]{:S(2)}) %collective-permute-start.4) | collective-permute-done | bytes 262176 | tf_op jit(solution)/shard_map/ppermute | solution.py:205
  38.5 0.1 fusion.7
  38.5 1.8 %collective-permute-start.5 = (bf16[2,32,1024]{2,1,0:T(8,128)(2,1)S(1)}, bf16[2,32,1024]{2,1,0:T(8,128)(2,1)S(1)}, u32[]{:S(2)}, u32[]{:S(2)}) collective-permute-start(bf16[2,32,1024]{2,1,0:T(8,128)(2,1)S(1)} %get-tuple-element.20), channel_id=1, source_target_pairs={{0,4},{1,5},{2,6},{3,7},{4,0},{5,1},{6,2},{7,3},{8,12},{9,13},{10,... | collective-permute-start | bytes 393224 | tf_op jit(solution)/shard_map/ppermute | solution.py:205
  40.4 1.4 %collective-permute-start.6 = (bf16[2,32,1024]{2,1,0:T(8,128)(2,1)S(1)}, bf16[2,32,1024]{2,1,0:T(8,128)(2,1)S(1)}, u32[]{:S(2)}, u32[]{:S(2)}) collective-permute-start(bf16[2,32,1024]{2,1,0:T(8,128)(2,1)S(1)} %get-tuple-element.21), channel_id=1, source_target_pairs={{0,6},{1,7},{2,4},{3,5},{4,2},{5,3},{6,0},{7,1},{8,14},{9,15},{10,... | collective-permute-start | bytes 393224 | tf_op jit(solution)/shard_map/ppermute | solution.py:205
  41.8 1.5 %collective-permute-start = (bf16[3,32,1024]{2,1,0:T(8,128)(2,1)S(1)}, bf16[3,32,1024]{2,1,0:T(8,128)(2,1)S(1)}, u32[]{:S(2)}, u32[]{:S(2)}) collective-permute-start(bf16[3,32,1024]{2,1,0:T(8,128)(2,1)S(1)} %get-tuple-element.10), channel_id=1, source_target_pairs={{0,4},{1,5},{2,6},{3,7},{4,0},{5,1},{6,2},{7,3},{8,12},{9,13},{10,... | collective-permute-start | bytes 589832 | tf_op jit(solution)/shard_map/ppermute | solution.py:205
  43.3 4.2 %collective-permute-done.5 = bf16[2,32,1024]{2,1,0:T(8,128)(2,1)S(1)} collective-permute-done((bf16[2,32,1024]{2,1,0:T(8,128)(2,1)S(1)}, bf16[2,32,1024]{2,1,0:T(8,128)(2,1)S(1)}, u32[]{:S(2)}, u32[]{:S(2)}) %collective-permute-start.5) | collective-permute-done | bytes 131104 | tf_op jit(solution)/shard_map/ppermute | solution.py:205
  47.5 0.0 collective-permute-done.6
  47.6 3.8 %collective-permute-done = bf16[3,32,1024]{2,1,0:T(8,128)(2,1)S(1)} collective-permute-done((bf16[3,32,1024]{2,1,0:T(8,128)(2,1)S(1)}, bf16[3,32,1024]{2,1,0:T(8,128)(2,1)S(1)}, u32[]{:S(2)}, u32[]{:S(2)}) %collective-permute-start) | collective-permute-done | bytes 196640 | tf_op jit(solution)/shard_map/ppermute | solution.py:205
  51.4 0.1 fusion
  51.6 0.7 %fusion.5 = (bf16[1,32,1024]{2,1,0:T(8,128)(2,1)}, bf16[1,32,1024]{2,1,0:T(8,128)(2,1)}) fusion(f32[2,32,1024]{2,1,0:T(8,128)S(1)} %convert_add_fusion, bf16[3,32,1024]{2,1,0:T(8,128)(2,1)S(1)} %collective-permute-done, f32[32]{0:T(128)S(1)} %get-tuple-element.25, f32[32]{0:T(128)S(1)} %get-tuple-element.24), kind=kLoop, calls=%fused_computation.11 | loop fusion | flops 425984 | bytes 590080 | tf_op jit(solution)/shard_map/convert_element_type | solution.py:261
  (2 shorter events, 0.0 us)
Async XLA Ops:
  1.7 6.5 %collective-permute-start.2 = (bf16[2,32,1024]{2,1,0:T(8,128)(2,1)S(1)}, bf16[2,32,1024]{2,1,0:T(8,128)(2,1)S(1)}, u32[]{:S(2)}, u32[]{:S(2)}) collective-permute-start(bf16[2,32,1024]{2,1,0:T(8,128)(2,1)S(1)} %get-tuple-element.11.refs_0_), channel_id=1, source_target_pairs={{0,2},{1,3},{2,0},{3,1},{4,6},{5,7},{6,4},{7,5},{8,10},{9,11},{10,... | collective-permute-start | bytes 393224 | tf_op jit(solution)/shard_map/ppermute | solution.py:205
  4.7 7.2 %collective-permute-start.1 = (bf16[2,32,1024]{2,1,0:T(8,128)(2,1)S(1)}, bf16[2,32,1024]{2,1,0:T(8,128)(2,1)S(1)}, u32[]{:S(2)}, u32[]{:S(2)}) collective-permute-start(bf16[2,32,1024]{2,1,0:T(8,128)(2,1)S(1)} %get-tuple-element.11.refs_0_), channel_id=1, source_target_pairs={{0,1},{1,0},{2,3},{3,2},{4,5},{5,4},{6,7},{7,6},{8,9},{9,8},{10,11... | collective-permute-start | bytes 393224 | tf_op jit(solution)/shard_map/ppermute | solution.py:205
  8.2 3.7 %collective-permute-start.3 = (bf16[2,32,1024]{2,1,0:T(8,128)(2,1)S(1)}, bf16[2,32,1024]{2,1,0:T(8,128)(2,1)S(1)}, u32[]{:S(2)}, u32[]{:S(2)}) collective-permute-start(bf16[2,32,1024]{2,1,0:T(8,128)(2,1)S(1)} %collective-permute-done.2.refs_2_), channel_id=1, source_target_pairs={{0,1},{1,0},{2,3},{3,2},{4,5},{5,4},{6,7},{7,6},{8,9},{9,8},{10,11... | collective-permute-start | bytes 393224 | tf_op jit(solution)/shard_map/ppermute | solution.py:205
  36.7 1.7 %collective-permute-start.4 = (bf16[2,2,32,1024]{3,2,1,0:T(8,128)(2,1)S(1)}, bf16[2,2,32,1024]{3,2,1,0:T(8,128)(2,1)S(1)}, u32[]{:S(2)}, u32[]{:S(2)}) collective-permute-start(bf16[2,2,32,1024]{3,2,1,0:T(8,128)(2,1)S(1)} %get-tuple-element.17), channel_id=1, source_target_pairs={{0,1},{1,0},{2,3},{3,2},{4,5},{5,4},{6,7},{7,6},{8,9},{9,8},{10,11... | collective-permute-start | bytes 786440 | tf_op jit(solution)/shard_map/ppermute | solution.py:205
  38.5 9.0 %collective-permute-start.5 = (bf16[2,32,1024]{2,1,0:T(8,128)(2,1)S(1)}, bf16[2,32,1024]{2,1,0:T(8,128)(2,1)S(1)}, u32[]{:S(2)}, u32[]{:S(2)}) collective-permute-start(bf16[2,32,1024]{2,1,0:T(8,128)(2,1)S(1)} %get-tuple-element.20), channel_id=1, source_target_pairs={{0,4},{1,5},{2,6},{3,7},{4,0},{5,1},{6,2},{7,3},{8,12},{9,13},{10,... | collective-permute-start | bytes 393224 | tf_op jit(solution)/shard_map/ppermute | solution.py:205
  40.4 7.2 %collective-permute-start.6 = (bf16[2,32,1024]{2,1,0:T(8,128)(2,1)S(1)}, bf16[2,32,1024]{2,1,0:T(8,128)(2,1)S(1)}, u32[]{:S(2)}, u32[]{:S(2)}) collective-permute-start(bf16[2,32,1024]{2,1,0:T(8,128)(2,1)S(1)} %get-tuple-element.21), channel_id=1, source_target_pairs={{0,6},{1,7},{2,4},{3,5},{4,2},{5,3},{6,0},{7,1},{8,14},{9,15},{10,... | collective-permute-start | bytes 393224 | tf_op jit(solution)/shard_map/ppermute | solution.py:205
  41.8 9.6 %collective-permute-start = (bf16[3,32,1024]{2,1,0:T(8,128)(2,1)S(1)}, bf16[3,32,1024]{2,1,0:T(8,128)(2,1)S(1)}, u32[]{:S(2)}, u32[]{:S(2)}) collective-permute-start(bf16[3,32,1024]{2,1,0:T(8,128)(2,1)S(1)} %get-tuple-element.10), channel_id=1, source_target_pairs={{0,4},{1,5},{2,6},{3,7},{4,0},{5,1},{6,2},{7,3},{8,12},{9,13},{10,... | collective-permute-start | bytes 589832 | tf_op jit(solution)/shard_map/ppermute | solution.py:205

commit v6 on v5

--- a/solution.py
+++ b/solution.py
@@ -244,10 +244,18 @@
     if size & (size - 1) == 0 and size > 1 and rows % 16 == 0:
         keep, give = section(tile, exchanged(own, size), scale, first, *arrays)
         got = sent(give, 0, 1)
-        total = jnp.zeros((2,) + own.shape[1:], F32)
+
+        def pair_sum(k, path):
+            return (keep[k, path].astype(F32) + got[k, path].astype(F32)).astype(BF16)
+
+        back = pair_sum(0, 1).astype(F32)
+        ahead = jnp.zeros(own.shape[1:], F32)
+        for k in range(1, size // 2):
+            back = back + sent(pair_sum(k, 1), 0, 2 * k).astype(F32)
         for k in range(size // 2):
-            pair = (keep[k].astype(F32) + got[k].astype(F32)).astype(BF16)
-            total = total + moved(pair, 2 * k).astype(F32)
+            ahead = ahead + sent(pair_sum(k, 0), 1, 2 * k).astype(F32)
+        back = sent(back.astype(BF16), -1, 0).astype(F32)
+        total = (ahead, back)
     else:
         whole = lax.all_gather(own, "mp", axis=1, tiled=True)
         (part,) = section(tile, [whole], scale, first, *arrays)

time: 52.5 us -> 52.3 us (level)
  waiting for transfers between devices: 12.7 us -> 9.25 us
  starting transfers between devices: 8.4 us -> 11.7 us
    ppermute x7 -> x9, waiting for transfers between devices: 12.7 us -> 9.25 us  [sent(): return lax.ppermute(block, ('pipe', 'mp'), route)]
    ppermute x7 -> x9, starting transfers between devices: 8.4 us -> 11.7 us  [sent(): return lax.ppermute(block, ('pipe', 'mp'), route)]
    broadcast_in_dim x0 -> x1, other arithmetic: none -> 0.74 us  [on_device(): return (section_out[None], input_grad[None])]
    convert_element_type x2, other arithmetic: 0.81 us -> 0.08 us  [the longest x1 0.05 us: pair_sum(): return (keep[k, path].astype(F32) + got[k, path].astype(F32)).astype(BF16)]
  transfers between devices with their start and end apart: 7 -> 9, of which waited for: 4 -> 6; matrix products, arithmetic and copies ran while one was open for 0% -> 0% of each run, Pallas kernels for 7% -> 7%
where the time goes in v6:
time: 52.3 us; the launch traced here: 52.2 us
  Pallas kernels  29.5 us (56%)
  starting transfers between devices  11.7 us (22%)
  waiting for transfers between devices  9.25 us (18%)
  other arithmetic  0.96 us (2%)
  between operations  0.7 us (1%)
    pallas_call x1, Pallas kernels, section(): pl.pallas_call(functools.partial(section_kernel, tiles, tile, depth, rows...  24.8 us
    ppermute x9, starting transfers between devices, sent(): return lax.ppermute(block, ('pipe', 'mp'), route)  11.7 us
    ppermute x9, waiting for transfers between devices, sent(): return lax.ppermute(block, ('pipe', 'mp'), route)  9.25 us
    pallas_call x1, Pallas kernels, first_tile(): pl.pallas_call(functools.partial(load_kernel, tile), in_specs=[pl.BlockSp...  3.67 us
  transfers between devices with their start and end apart: 9, of which 6 were waited for; matrix products, arithmetic and copies ran while one was open for 0% of the time, Pallas kernels for 7%

profile of v6, /device:TPU:0, one launch (start us, length us, event | category | flops | bytes accessed | tf_op | source)
XLA Modules:
  0.0 52.2 jit_solution(4691019077220496694)
XLA Ops:
  0.6 1.0 %pack.1 = (bf16[2,32,1024]{2,1,0:T(8,128)(2,1)S(1)}, bf16[3,32,1024]{2,1,0:T(8,128)(2,1)S(1)}, f32[1,1024]{1,0:T(1,128)S(1)}) custom-call(bf16[32,1024]{1,0:T(8,128)(2,1)} %bitcast.46, bf16[32,1024]{1,0:T(8,128)(2,1)} %bitcast.47, bf16[32,1024]{1,0:T(8,128)(2,1)} %bitcast.48, f32[1,1024]{1,0:T(1,128)} %gain_ref.1), custom_call_target="tpu_custom_call" | custom-call | tf_op jit(solution)/shard_map/pack/pallas_call | solution.py:35
  1.7 3.0 %collective-permute-start.2 = (bf16[2,32,1024]{2,1,0:T(8,128)(2,1)S(1)}, bf16[2,32,1024]{2,1,0:T(8,128)(2,1)S(1)}, u32[]{:S(2)}, u32[]{:S(2)}) collective-permute-start(bf16[2,32,1024]{2,1,0:T(8,128)(2,1)S(1)} %get-tuple-element.11.refs_0_), channel_id=1, source_target_pairs={{0,2},{1,3},{2,0},{3,1},{4,6},{5,7},{6,4},{7,5},{8,10},{9,11},{10,... | collective-permute-start | bytes 393224 | tf_op jit(solution)/shard_map/ppermute | solution.py:205
  4.7 0.0 collective-permute-start.1
  4.7 3.5 %collective-permute-done.2.refs_2_ = bf16[2,32,1024]{2,1,0:T(8,128)(2,1)S(1)} collective-permute-done((bf16[2,32,1024]{2,1,0:T(8,128)(2,1)S(1)}, bf16[2,32,1024]{2,1,0:T(8,128)(2,1)S(1)}, u32[]{:S(2)}, u32[]{:S(2)}) %collective-permute-start.2) | collective-permute-done | bytes 131104 | tf_op jit(solution)/shard_map/ppermute | solution.py:205
  8.2 0.0 collective-permute-start.3
  8.2 3.7 %load.1 = (bf16[128,2048]{1,0:T(8,128)(2,1)S(1)}, bf16[1024,2048]{1,0:T(8,128)(2,1)S(1)}, bf16[2048,1024]{1,0:T(8,128)(2,1)S(1)}) custom-call(bf16[128,16384]{1,0:T(8,128)(2,1)} %bitcast.44, bf16[1024,16384]{1,0:T(8,128)(2,1)} %bitcast.40, bf16[16384,1024]{1,0:T(8,128)(2,1)} %bitcast.42), custom_call_target="tpu_custom_call" | custom-call | bytes 17825792 | tf_op jit(solution)/shard_map/load/pallas_call | solution.py:67
  11.9 0.0 collective-permute-done.1.refs_1_
  11.9 0.0 collective-permute-done.3.refs_3_
  11.9 24.8 %section.1 = (bf16[2,2,32,1024]{3,2,1,0:T(8,128)(2,1)S(1)}, bf16[2,2,32,1024]{3,2,1,0:T(8,128)(2,1)S(1)}) custom-call(bf16[2,32,1024]{2,1,0:T(8,128)(2,1)S(1)} %get-tuple-element.11.refs_0_, bf16[2,32,1024]{2,1,0:T(8,128)(2,1)S(1)} %collective-permute-done.1.refs_1_, bf16[2,32,1024]{2,1,0:T(8,128)(2,1)S(1)} %collective-permute-done.2.refs_2_, ...), custom_call_target="tpu_custom_call" | custom-call | flops 17179869184 | bytes 71303168 | tf_op jit(solution)/shard_map/section/pallas_call | solution.py:165
  36.7 0.6 %collective-permute-start.4 = (bf16[2,2,32,1024]{3,2,1,0:T(8,128)(2,1)S(1)}, bf16[2,2,32,1024]{3,2,1,0:T(8,128)(2,1)S(1)}, u32[]{:S(2)}, u32[]{:S(2)}) collective-permute-start(bf16[2,2,32,1024]{3,2,1,0:T(8,128)(2,1)S(1)} %get-tuple-element.17), channel_id=1, source_target_pairs={{0,1},{1,0},{2,3},{3,2},{4,5},{5,4},{6,7},{7,6},{8,9},{9,8},{10,11... | collective-permute-start | bytes 786440 | tf_op jit(solution)/shard_map/ppermute | solution.py:205
  37.3 1.2 %collective-permute-done.4 = bf16[2,2,32,1024]{3,2,1,0:T(8,128)(2,1)S(1)} collective-permute-done((bf16[2,2,32,1024]{3,2,1,0:T(8,128)(2,1)S(1)}, bf16[2,2,32,1024]{3,2,1,0:T(8,128)(2,1)S(1)}, u32[]{:S(2)}, u32[]{:S(2)}) %collective-permute-start.4) | collective-permute-done | bytes 262176 | tf_op jit(solution)/shard_map/ppermute | solution.py:205
  38.5 1.8 %collective-permute-start.7 = (bf16[32,1024]{1,0:T(8,128)(2,1)S(1)}, bf16[32,1024]{1,0:T(8,128)(2,1)S(1)}, u32[]{:S(2)}, u32[]{:S(2)}) collective-permute-start(bf16[32,1024]{1,0:T(8,128)(2,1)S(1)} %get-tuple-element.20), channel_id=1, source_target_pairs={{0,2},{1,3},{2,0},{3,1},{4,6},{5,7},{6,4},{7,5},{8,10},{9,11},{10,... | collective-permute-start | bytes 196616 | tf_op jit(solution)/shard_map/ppermute | solution.py:205
  40.3 1.5 %collective-permute-start = (bf16[3,32,1024]{2,1,0:T(8,128)(2,1)S(1)}, bf16[3,32,1024]{2,1,0:T(8,128)(2,1)S(1)}, u32[]{:S(2)}, u32[]{:S(2)}) collective-permute-start(bf16[3,32,1024]{2,1,0:T(8,128)(2,1)S(1)} %get-tuple-element.10), channel_id=1, source_target_pairs={{0,4},{1,5},{2,6},{3,7},{4,0},{5,1},{6,2},{7,3},{8,12},{9,13},{10,... | collective-permute-start | bytes 589832 | tf_op jit(solution)/shard_map/ppermute | solution.py:205
  41.8 1.1 %collective-permute-done.7 = bf16[32,1024]{1,0:T(8,128)(2,1)S(1)} collective-permute-done((bf16[32,1024]{1,0:T(8,128)(2,1)S(1)}, bf16[32,1024]{1,0:T(8,128)(2,1)S(1)}, u32[]{:S(2)}, u32[]{:S(2)}) %collective-permute-start.7) | collective-permute-done | bytes 65568 | tf_op jit(solution)/shard_map/ppermute | solution.py:205
  43.0 1.8 %collective-permute-start.8 = (bf16[32,1024]{1,0:T(8,128)(2,1)S(1)}, bf16[32,1024]{1,0:T(8,128)(2,1)S(1)}, u32[]{:S(2)}, u32[]{:S(2)}) collective-permute-start(bf16[32,1024]{1,0:T(8,128)(2,1)S(1)} %fusion.8), channel_id=1, source_target_pairs={{0,4},{1,5},{2,6},{3,7},{4,0},{5,1},{6,2},{7,3},{8,12},{9,13},{10,... | collective-permute-start | bytes 196616 | tf_op jit(solution)/shard_map/ppermute | solution.py:205
  44.8 1.4 %collective-permute-start.6 = (bf16[32,1024]{1,0:T(8,128)(2,1)S(1)}, bf16[32,1024]{1,0:T(8,128)(2,1)S(1)}, u32[]{:S(2)}, u32[]{:S(2)}) collective-permute-start(bf16[32,1024]{1,0:T(8,128)(2,1)S(1)} %get-tuple-element.21), channel_id=1, source_target_pairs={{0,6},{1,7},{2,4},{3,5},{4,2},{5,3},{6,0},{7,1},{8,14},{9,15},{10,... | collective-permute-start | bytes 196616 | tf_op jit(solution)/shard_map/ppermute | solution.py:205
  46.2 1.5 %collective-permute-start.5 = (bf16[32,1024]{1,0:T(8,128)(2,1)S(1)}, bf16[32,1024]{1,0:T(8,128)(2,1)S(1)}, u32[]{:S(2)}, u32[]{:S(2)}) collective-permute-start(bf16[32,1024]{1,0:T(8,128)(2,1)S(1)} %get-tuple-element.22), channel_id=1, source_target_pairs={{0,4},{1,5},{2,6},{3,7},{4,0},{5,1},{6,2},{7,3},{8,12},{9,13},{10,... | collective-permute-start | bytes 196616 | tf_op jit(solution)/shard_map/ppermute | solution.py:205
  47.8 1.0 %collective-permute-done = bf16[3,32,1024]{2,1,0:T(8,128)(2,1)S(1)} collective-permute-done((bf16[3,32,1024]{2,1,0:T(8,128)(2,1)S(1)}, bf16[3,32,1024]{2,1,0:T(8,128)(2,1)S(1)}, u32[]{:S(2)}, u32[]{:S(2)}) %collective-permute-start) | collective-permute-done | bytes 196640 | tf_op jit(solution)/shard_map/ppermute | solution.py:205
  48.8 1.9 %collective-permute-done.8 = bf16[32,1024]{1,0:T(8,128)(2,1)S(1)} collective-permute-done((bf16[32,1024]{1,0:T(8,128)(2,1)S(1)}, bf16[32,1024]{1,0:T(8,128)(2,1)S(1)}, u32[]{:S(2)}, u32[]{:S(2)}) %collective-permute-start.8) | collective-permute-done | bytes 65568 | tf_op jit(solution)/shard_map/ppermute | solution.py:205
  50.7 0.1 fusion.3
  50.9 0.0 collective-permute-done.6
  50.9 0.5 %collective-permute-done.5 = bf16[32,1024]{1,0:T(8,128)(2,1)S(1)} collective-permute-done((bf16[32,1024]{1,0:T(8,128)(2,1)S(1)}, bf16[32,1024]{1,0:T(8,128)(2,1)S(1)}, u32[]{:S(2)}, u32[]{:S(2)}) %collective-permute-start.5) | collective-permute-done | bytes 65568 | tf_op jit(solution)/shard_map/ppermute | solution.py:205
  51.4 0.7 %fusion.15 = (bf16[1,32,1024]{2,1,0:T(8,128)(2,1)}, bf16[1,32,1024]{2,1,0:T(8,128)(2,1)}) fusion(bf16[32,1024]{1,0:T(8,128)(2,1)S(1)} %collective-permute-done.8, bf16[3,32,1024]{2,1,0:T(8,128)(2,1)S(1)} %collective-permute-done, f32[32]{0:T(128)S(1)} %get-tuple-element.26, f32[32]{0:T(128)S(1)} %get-tuple-element.25, ...), kind=kLoop, calls=%fused_computation.25 | loop fusion | flops 557056 | bytes 524544 | tf_op jit(solution)/shard_map/broadcast_in_dim | solution.py:270
  (3 shorter events, 0.1 us)
Async XLA Ops:
  1.7 6.5 %collective-permute-start.2 = (bf16[2,32,1024]{2,1,0:T(8,128)(2,1)S(1)}, bf16[2,32,1024]{2,1,0:T(8,128)(2,1)S(1)}, u32[]{:S(2)}, u32[]{:S(2)}) collective-permute-start(bf16[2,32,1024]{2,1,0:T(8,128)(2,1)S(1)} %get-tuple-element.11.refs_0_), channel_id=1, source_target_pairs={{0,2},{1,3},{2,0},{3,1},{4,6},{5,7},{6,4},{7,5},{8,10},{9,11},{10,... | collective-permute-start | bytes 393224 | tf_op jit(solution)/shard_map/ppermute | solution.py:205
  4.7 7.2 %collective-permute-start.1 = (bf16[2,32,1024]{2,1,0:T(8,128)(2,1)S(1)}, bf16[2,32,1024]{2,1,0:T(8,128)(2,1)S(1)}, u32[]{:S(2)}, u32[]{:S(2)}) collective-permute-start(bf16[2,32,1024]{2,1,0:T(8,128)(2,1)S(1)} %get-tuple-element.11.refs_0_), channel_id=1, source_target_pairs={{0,1},{1,0},{2,3},{3,2},{4,5},{5,4},{6,7},{7,6},{8,9},{9,8},{10,11... | collective-permute-start | bytes 393224 | tf_op jit(solution)/shard_map/ppermute | solution.py:205
  8.2 3.7 %collective-permute-start.3 = (bf16[2,32,1024]{2,1,0:T(8,128)(2,1)S(1)}, bf16[2,32,1024]{2,1,0:T(8,128)(2,1)S(1)}, u32[]{:S(2)}, u32[]{:S(2)}) collective-permute-start(bf16[2,32,1024]{2,1,0:T(8,128)(2,1)S(1)} %collective-permute-done.2.refs_2_), channel_id=1, source_target_pairs={{0,1},{1,0},{2,3},{3,2},{4,5},{5,4},{6,7},{7,6},{8,9},{9,8},{10,11... | collective-permute-start | bytes 393224 | tf_op jit(solution)/shard_map/ppermute | solution.py:205
  36.7 1.7 %collective-permute-start.4 = (bf16[2,2,32,1024]{3,2,1,0:T(8,128)(2,1)S(1)}, bf16[2,2,32,1024]{3,2,1,0:T(8,128)(2,1)S(1)}, u32[]{:S(2)}, u32[]{:S(2)}) collective-permute-start(bf16[2,2,32,1024]{3,2,1,0:T(8,128)(2,1)S(1)} %get-tuple-element.17), channel_id=1, source_target_pairs={{0,1},{1,0},{2,3},{3,2},{4,5},{5,4},{6,7},{7,6},{8,9},{9,8},{10,11... | collective-permute-start | bytes 786440 | tf_op jit(solution)/shard_map/ppermute | solution.py:205
  38.5 4.4 %collective-permute-start.7 = (bf16[32,1024]{1,0:T(8,128)(2,1)S(1)}, bf16[32,1024]{1,0:T(8,128)(2,1)S(1)}, u32[]{:S(2)}, u32[]{:S(2)}) collective-permute-start(bf16[32,1024]{1,0:T(8,128)(2,1)S(1)} %get-tuple-element.20), channel_id=1, source_target_pairs={{0,2},{1,3},{2,0},{3,1},{4,6},{5,7},{6,4},{7,5},{8,10},{9,11},{10,... | collective-permute-start | bytes 196616 | tf_op jit(solution)/shard_map/ppermute | solution.py:205
  40.3 8.5 %collective-permute-start = (bf16[3,32,1024]{2,1,0:T(8,128)(2,1)S(1)}, bf16[3,32,1024]{2,1,0:T(8,128)(2,1)S(1)}, u32[]{:S(2)}, u32[]{:S(2)}) collective-permute-start(bf16[3,32,1024]{2,1,0:T(8,128)(2,1)S(1)} %get-tuple-element.10), channel_id=1, source_target_pairs={{0,4},{1,5},{2,6},{3,7},{4,0},{5,1},{6,2},{7,3},{8,12},{9,13},{10,... | collective-permute-start | bytes 589832 | tf_op jit(solution)/shard_map/ppermute | solution.py:205
  43.0 7.7 %collective-permute-start.8 = (bf16[32,1024]{1,0:T(8,128)(2,1)S(1)}, bf16[32,1024]{1,0:T(8,128)(2,1)S(1)}, u32[]{:S(2)}, u32[]{:S(2)}) collective-permute-start(bf16[32,1024]{1,0:T(8,128)(2,1)S(1)} %fusion.8), channel_id=1, source_target_pairs={{0,4},{1,5},{2,6},{3,7},{4,0},{5,1},{6,2},{7,3},{8,12},{9,13},{10,... | collective-permute-start | bytes 196616 | tf_op jit(solution)/shard_map/ppermute | solution.py:205
  44.8 6.1 %collective-permute-start.6 = (bf16[32,1024]{1,0:T(8,128)(2,1)S(1)}, bf16[32,1024]{1,0:T(8,128)(2,1)S(1)}, u32[]{:S(2)}, u32[]{:S(2)}) collective-permute-start(bf16[32,1024]{1,0:T(8,128)(2,1)S(1)} %get-tuple-element.21), channel_id=1, source_target_pairs={{0,6},{1,7},{2,4},{3,5},{4,2},{5,3},{6,0},{7,1},{8,14},{9,15},{10,... | collective-permute-start | bytes 196616 | tf_op jit(solution)/shard_map/ppermute | solution.py:205
  46.2 5.2 %collective-permute-start.5 = (bf16[32,1024]{1,0:T(8,128)(2,1)S(1)}, bf16[32,1024]{1,0:T(8,128)(2,1)S(1)}, u32[]{:S(2)}, u32[]{:S(2)}) collective-permute-start(bf16[32,1024]{1,0:T(8,128)(2,1)S(1)} %get-tuple-element.22), channel_id=1, source_target_pairs={{0,4},{1,5},{2,6},{3,7},{4,0},{5,1},{6,2},{7,3},{8,12},{9,13},{10,... | collective-permute-start | bytes 196616 | tf_op jit(solution)/shard_map/ppermute | solution.py:205
